TPU v7x, 512 devices: a whole 4x4x16 slice. The times are simulated.
512 devices in a mesh: rep: 64 (over x_lo, z, core), tp: 8 (over y, x_hi).
Axes of the slice: x: 4 (x_hi: 2, x_lo: 2; x = x_hi * 2 + x_lo), y: 4, z: 16, core: 2. Of those that a mesh axis runs over, the one named last changes fastest.
Arguments:
- prompt_q: bfloat16 [32768, 2048], P('rep', 'tp'), may hold values from -24 to 24
- prompt_k: bfloat16 [32768, 2048], P('rep', 'tp'), may hold values from -24 to 24
- prompt_v: bfloat16 [32768, 2048], P('rep', 'tp'), may hold values from -6 to 6
- prompt_len: int32 [64], P('rep'), may hold values from 256 to 512, as said below
- cache_keys: bfloat16 [128, 1024, 2048], P('rep', None, 'tp'), may hold values from -24 to 24
- cache_values: bfloat16 [128, 1024, 2048], P('rep', None, 'tp'), may hold values from -6 to 6
- new_q: bfloat16 [128, 2048], P('rep', 'tp'), may hold values from -24 to 24
- new_k: bfloat16 [128, 2048], P('rep', 'tp'), may hold values from -6 to 6
- new_v: bfloat16 [128, 2048], P('rep', 'tp'), may hold values from -6 to 6
- cache_len: int32 [128], replicated, may hold values from 260 to 1024, as said below
- moving: int32 [64], replicated, may hold values from 0 to 1
- out_weight: bfloat16 [2048, 2048], P(None, 'tp'), may hold values from -0.125 to 0.125
- out_bias: float32 [2048], P('tp'), may hold values from -1.75 to 1.75
- residual: bfloat16 [32896, 2048], P('rep', 'tp'), may hold values from -150 to 150
- ln_gain: float32 [2048], P('tp'), may hold values from 0.1 to 1.9
- ln_shift: float32 [2048], P('tp'), may hold values from -1.75 to 1.75
Outputs:
- hidden_out: bfloat16 [32896, 2048], P('rep', 'tp')
- normed: bfloat16 [32896, 2048], P('rep', 'tp')
- moved_window: bfloat16 [64, 2, 260, 2048], P('rep', None, None, 'tp')
Inputs may be any that keep to these rules, and one draw needn't show every extreme that they name: `prompt_len`: some replica's prompt has all 512 tokens live. `cache_len`: some request's cache is full.
All inputs are finite; a program needn't handle non-finite values.
Results may differ from a plain program's by a relative error of at most 0.0022.
Values may be sent and summed in bfloat16 or wider, within the bound.
No kernel may reach another device: no remote copies, remote signals or barrier semaphores. Data moves between devices by JAX's collectives and lax.ppermute only.
A program may use at most 64 MiB of HBM per device.

v0:
```python
import math

import jax
import jax.numpy as jnp
from jax import lax
from jax.sharding import PartitionSpec as P

D = 2048
HEADS = 16
HD = 128
SINK = 4
WIN = 256


masked_score = -1e30
norm_epsilon = 1e-05


def from_behind(block, axis, distance):
    devices = range(lax.axis_size(axis))
    route = [((i - distance) % len(devices), i) for i in devices]
    return lax.ppermute(block, axis, route)


def head_slopes(local_heads):
    first_head = lax.axis_index("tp") * local_heads
    head_ids = (first_head + jnp.arange(local_heads, dtype=jnp.int32)).astype(jnp.float32)
    return jnp.exp2(-8.0 * (head_ids + 1.0) / HEADS)


def softmax_rows(scores):
    row_max = jnp.max(scores, axis=-1, keepdims=True)
    expo_terms = jnp.exp(scores - row_max)
    return (expo_terms / jnp.sum(expo_terms, axis=-1, keepdims=True)).astype(jnp.bfloat16)


def prompt_attend(query_rows, key_rows, value_rows, length, slopes):
    row_count = query_rows.shape[0]
    local_heads = slopes.shape[0]
    query_heads = query_rows.reshape(row_count, local_heads, HD)
    key_heads = key_rows.reshape(row_count, local_heads, HD)
    value_heads = value_rows.reshape(row_count, local_heads, HD)
    scores = jnp.einsum(
        "qhd,khd->hqk", query_heads, key_heads, preferred_element_type=jnp.float32
    ) * (1.0 / math.sqrt(HD))
    position = jnp.arange(row_count, dtype=jnp.int32)
    distance = (position[:, None] - position[None, :]).astype(jnp.float32)
    scores = scores - slopes[:, None, None] * distance[None]
    allowed = (position[None, :] <= position[:, None]) & (position[None, :] < length)
    scores = jnp.where(allowed[None], scores, masked_score)
    weights = softmax_rows(scores)
    mixed_heads = jnp.einsum(
        "hqk,khd->qhd", weights, value_heads, preferred_element_type=jnp.float32
    )
    return mixed_heads.astype(jnp.bfloat16).reshape(row_count, local_heads * HD)


def window_rows(cache_rows, newest, length):
    middle = lax.dynamic_slice_in_dim(cache_rows, length + 1 - WIN, WIN - 1, 0)
    return jnp.concatenate([cache_rows[:SINK], middle, newest[None]], axis=0)


def window_positions(length):
    sink_part = jnp.arange(SINK, dtype=jnp.int32)
    tail_part = length + 1 - WIN + jnp.arange(WIN, dtype=jnp.int32)
    return jnp.concatenate([sink_part, tail_part])


def decode_attend(query_row, key_window, value_window, length, slopes):
    local_heads = slopes.shape[0]
    query_heads = query_row.reshape(local_heads, HD)
    key_heads = key_window.reshape(-1, local_heads, HD)
    value_heads = value_window.reshape(-1, local_heads, HD)
    scores = jnp.einsum(
        "hd,whd->hw", query_heads, key_heads, preferred_element_type=jnp.float32
    ) * (1.0 / math.sqrt(HD))
    distance = (length - window_positions(length)).astype(jnp.float32)
    scores = scores - slopes[:, None] * distance[None, :]
    weights = softmax_rows(scores)
    mixed_heads = jnp.einsum("hw,whd->hd", weights, value_heads, preferred_element_type=jnp.float32)
    return mixed_heads.astype(jnp.bfloat16).reshape(local_heads * HD)


def select_slot(stacked, slot_index):
    return lax.dynamic_index_in_dim(stacked, slot_index, 0, keepdims=False)


def on_device(
    prompt_q,
    prompt_k,
    prompt_v,
    prompt_len,
    cache_keys,
    cache_values,
    new_q,
    new_k,
    new_v,
    cache_len,
    moving,
    out_weight,
    out_bias,
    residual,
    ln_gain,
    ln_shift,
):
    replica_count = lax.axis_size("rep")
    replica_index = lax.axis_index("rep")
    partner = (replica_index + replica_count // 2) % replica_count
    local_heads = prompt_q.shape[1] // HD
    slopes = head_slopes(local_heads)
    prompt_mix = prompt_attend(prompt_q, prompt_k, prompt_v, prompt_len[0], slopes)
    slot_count = cache_keys.shape[0]
    leaving = moving[replica_index]
    staying = 1 - leaving
    stay_len = cache_len[replica_index * slot_count + staying]
    come_len = cache_len[partner * slot_count + moving[partner]]
    stay_keys = window_rows(select_slot(cache_keys, staying), select_slot(new_k, staying), stay_len)
    stay_values = window_rows(
        select_slot(cache_values, staying), select_slot(new_v, staying), stay_len
    )
    stay_out = decode_attend(select_slot(new_q, staying), stay_keys, stay_values, stay_len, slopes)
    come_cache_keys, come_cache_values, come_query, come_key, come_value = from_behind(
        (
            select_slot(cache_keys, leaving),
            select_slot(cache_values, leaving),
            select_slot(new_q, leaving),
            select_slot(new_k, leaving),
            select_slot(new_v, leaving),
        ),
        "rep",
        replica_count // 2,
    )
    come_keys = window_rows(come_cache_keys, come_key, come_len)
    come_values = window_rows(come_cache_values, come_value, come_len)
    come_out = decode_attend(come_query, come_keys, come_values, come_len, slopes)
    mixed_rows = jnp.concatenate([prompt_mix, stay_out[None], come_out[None]], axis=0)
    projected = jnp.dot(
        lax.all_gather(mixed_rows, "tp", axis=1, tiled=True),
        out_weight,
        preferred_element_type=jnp.float32,
    )
    stream = projected + out_bias[None, :] + residual.astype(jnp.float32)
    hidden_out = stream.astype(jnp.bfloat16)
    row_total = jnp.sum(stream, axis=1)
    row_mean = lax.psum(row_total, "tp") / D
    centered = stream - row_mean[:, None]
    row_var = lax.psum(jnp.sum(centered * centered, axis=1), "tp") / D
    normed = (
        centered * lax.rsqrt(row_var + norm_epsilon)[:, None] * ln_gain[None, :] + ln_shift[None, :]
    ).astype(jnp.bfloat16)
    moved_window = jnp.stack([come_keys, come_values], axis=0)[None]
    return (hidden_out, normed, moved_window)


def solution(mesh):
    in_specs = (
        P("rep", "tp"),
        P("rep", "tp"),
        P("rep", "tp"),
        P("rep"),
        P("rep", None, "tp"),
        P("rep", None, "tp"),
        P("rep", "tp"),
        P("rep", "tp"),
        P("rep", "tp"),
        P(),
        P(),
        P(None, "tp"),
        P("tp"),
        P("rep", "tp"),
        P("tp"),
        P("tp"),
    )
    out_specs = (P("rep", "tp"), P("rep", "tp"), P("rep", None, None, "tp"))
    return jax.shard_map(
        on_device, mesh=mesh, in_specs=in_specs, out_specs=out_specs, check_vma=False
    )
```

profile of v0, /device:TPU:32, one launch (start us, length us, event | category | flops | bytes accessed | tf_op | source)
XLA Modules:
  0.0 192.9 jit_solution(14140378695549050792)
XLA Ops:
  7.3 1.3 fusion.47
  10.6 1.1 dynamic-slice_bitcast_fusion.1
  11.6 3.4 %collective-permute-start.1 = (bf16[1024,256]{1,0:T(8,128)(2,1)S(1)}, bf16[1024,256]{1,0:T(8,128)(2,1)}, u32[]{:S(2)}, u32[]{:S(2)}) collective-permute-start(bf16[1024,256]{1,0:T(8,128)(2,1)S(1)} %dynamic-slice_bitcast_fusion.1), channel_id=1, source_target_pairs={{256,0},{264,8},{272,16},{280,24},{288,32},{296,40},{304,48},{312,... | collective-permute-start | bytes 1572872 | tf_op jit(solution)/shard_map/ppermute | solution.py:22
  16.3 1.4 fusion.33
  17.7 2.4 %collective-permute-start.2 = (bf16[256]{0:T(256)(128)(2,1)}, bf16[256]{0:T(256)(128)(2,1)}, u32[]{:S(2)}, u32[]{:S(2)}) collective-permute-start(bf16[256]{0:T(256)(128)(2,1)} %get-tuple-element.10), channel_id=1, source_target_pairs={{256,0},{264,8},{272,16},{280,24},{288,32},{296,40},{304,48},{312,... | collective-permute-start | bytes 1544 | tf_op jit(solution)/shard_map/ppermute | solution.py:22
  20.2 1.2 fusion.35
  21.4 3.4 %collective-permute-start = (bf16[256]{0:T(256)(128)(2,1)}, bf16[256]{0:T(256)(128)(2,1)}, u32[]{:S(2)}, u32[]{:S(2)}) collective-permute-start(bf16[256]{0:T(256)(128)(2,1)} %fusion.35), channel_id=1, source_target_pairs={{256,0},{264,8},{272,16},{280,24},{288,32},{296,40},{304,48},{312,... | collective-permute-start | bytes 1544 | tf_op jit(solution)/shard_map/ppermute | solution.py:22
  24.8 1.1 dynamic-slice_bitcast_fusion
  25.9 2.4 %collective-permute-start.3 = (bf16[1024,256]{1,0:T(8,128)(2,1)S(1)}, bf16[1024,256]{1,0:T(8,128)(2,1)}, u32[]{:S(2)}, u32[]{:S(2)}) collective-permute-start(bf16[1024,256]{1,0:T(8,128)(2,1)S(1)} %dynamic-slice_bitcast_fusion), channel_id=1, source_target_pairs={{256,0},{264,8},{272,16},{280,24},{288,32},{296,40},{304,48},{312,... | collective-permute-start | bytes 1572872 | tf_op jit(solution)/shard_map/ppermute | solution.py:22
  28.3 0.6 fusion.34
  28.9 3.4 %collective-permute-start.4 = (bf16[256]{0:T(256)(128)(2,1)}, bf16[256]{0:T(256)(128)(2,1)}, u32[]{:S(2)}, u32[]{:S(2)}) collective-permute-start(bf16[256]{0:T(256)(128)(2,1)} %get-tuple-element.12), channel_id=1, source_target_pairs={{256,0},{264,8},{272,16},{280,24},{288,32},{296,40},{304,48},{312,... | collective-permute-start | bytes 1544 | tf_op jit(solution)/shard_map/ppermute | solution.py:22
  33.0 0.6 fusion.46
  36.0 0.7 constant_dynamic-slice_fusion.10
  36.7 0.6 iota_add_fusion
  37.3 0.7 constant_dynamic-slice_fusion.7
  38.1 1.0 constant_dynamic-slice_fusion.6
  39.3 0.2 pad_maximum_fusion.1
  39.5 0.1 fusion.13
  39.7 0.6 multiply_exponential_fusion
  41.1 0.1 fusion.2
  41.2 1.8 copy.50
  43.0 2.0 %fusion.24 = (f32[260]{0:T(512)S(1)}, f32[260]{0:T(512)S(1)}) fusion(s32[4]{0:T(128)S(1)} %iota.55, s32[256]{0:T(256)} %get-tuple-element.30, s32[]{:T(128)} %bitcast.6, s32[256]{0:T(256)} %get-tuple-element.29, s32[]{:T(128)} %bitcast.15), kind=kLoop, calls=%fused_computation.60 | loop fusion | flops 1560 | bytes 4152 | tf_op jit(solution)/shard_map/convert_element_type | solution.py:77
  45.0 1.5 pad_maximum_fusion.2
  46.5 3.0 %subtract_select_fusion = f32[2,512,512]{1,2,0:T(8,128)} fusion(f32[512,512]{0,1:T(8,128)S(1)} %subtract_convert_fusion, f32[2]{0:T(128)} %multiply_exponential_fusion, pred[512,512]{0,1:T(8,128)(4,1)S(1)} %fusion.2, bf16[512,256]{1,0:T(8,128)(2,1)} %param.17, bf16[512,256]{1,0:T(8,128)(2,1)} %param.16), kind=kOutput, calls=%fused_computation.3 | convolution fusion | flops 136314880 | bytes 3932168 | tf_op jit(solution)/shard_map/qhd,khd->hqk/dot_general | solution.py:43
  49.5 2.0 %fusion.48 = f32[2,512]{1,0:T(2,128)S(1)} fusion(f32[512,512]{0,1:T(8,128)S(1)} %subtract_convert_fusion, f32[2]{0:T(128)S(1)} %copy-done.4, pred[512,512]{0,1:T(8,128)(4,1)S(1)} %fusion.2, bf16[512,256]{1,0:T(8,128)(2,1)} %param.17, bf16[512,256]{1,0:T(8,128)(2,1)} %param.16), kind=kOutput, calls=%fused_computation.90 | convolution fusion | flops 137363968 | bytes 1839112 | tf_op jit(solution)/shard_map/sub | solution.py:33
  51.6 3.0 %convolution_convert_fusion = bf16[2,512,128]{1,2,0:T(8,128)(2,1)S(1)} fusion(bf16[512,2,128]{0,2,1:T(8,128)(2,1)} %bitcast.98, f32[2,512]{1,0:T(2,128)S(1)} %fusion.48, f32[2,512,512]{1,2,0:T(8,128)} %subtract_select_fusion), kind=kOutput, calls=%fused_computation.6 | convolution fusion | flops 135923200 | bytes 2625536 | tf_op jit(solution)/shard_map/hqk,khd->qhd/dot_general | solution.py:52
  54.6 0.9 constant_dynamic-slice_fusion.3
  55.7 0.7 slice.18
  56.4 0.8 pad_maximum_fusion.3
  57.2 0.8 fusion.9
  57.9 0.2 fusion.42
  58.2 0.2 fusion.27
  58.6 0.2 fusion.28
  58.9 0.9 constant_dynamic-slice_fusion.1
  59.8 0.1 copy.54
  60.1 0.7 slice.19
  60.8 0.8 pad_maximum_fusion.4
  61.8 0.1 copy.56
  61.9 0.8 pad_maximum_fusion
  62.8 0.6 broadcast_in_dim.20
  63.3 0.6 broadcast_in_dim.21
  64.1 0.9 copy.36
  65.0 75.5 %all-gather.2.cloned.1.call-done = bf16[514,2048]{0,1:T(8,128)(2,1)} async-done(((bf16[514,256]{0,1:T(8,128)(2,1)}), bf16[514,2048]{0,1:T(8,128)(2,1)}) %all-gather.2.cloned.1.call-update) | async-done | bytes 2105360 | tf_op jit(solution)/shard_map/all_gather | solution.py:138
  140.5 2.7 %fusion.53 = (f32[514]{0:T(1024)S(1)}, f32[514,256]{1,0:T(8,128)S(1)}) fusion(bf16[514,256]{1,0:T(8,128)(2,1)S(1)} %copy-done.8, f32[256]{0:T(256)S(1)} %copy-done.9, bf16[514,2048]{0,1:T(8,128)(2,1)} %all-gather.2.cloned.1.call-done, bf16[2048,256]{1,0:T(8,128)(2,1)S(1)} %copy-done), kind=kOutput, calls=%fused_computation.91 | convolution fusion | flops 539493888 | bytes 3946504 | tf_op jit(solution)/shard_map/dot_general | solution.py:137
  143.2 19.9 %psum.14 = f32[514]{0:T(1024)S(1)} all-reduce(f32[514]{0:T(1024)S(1)} %get-tuple-element.27), channel_id=1, replica_groups=mesh['rep'=64,'tp'=8] {'tp'}, use_global_device_ids=true, to_apply=%region_7.8 | all-reduce | flops 514 | bytes 4112 | tf_op jit(solution)/shard_map/psum | solution.py:145
  163.1 0.3 multiply_reduce_fusion
  163.3 21.7 %psum.15 = f32[514]{0:T(1024)S(1)} all-reduce(f32[514]{0:T(1024)S(1)} %multiply_reduce_fusion), channel_id=1, replica_groups=mesh['rep'=64,'tp'=8] {'tp'}, use_global_device_ids=true, to_apply=%region_9.10 | all-reduce | flops 514 | bytes 4112 | tf_op jit(solution)/shard_map/psum | solution.py:147
  185.1 1.0 add_convert_fusion
  (51 shorter events, 1.4 us)
Async XLA Ops:
  7.2 133.3 %copy-start = (bf16[2048,256]{1,0:T(8,128)(2,1)S(1)}, bf16[2048,256]{1,0:T(8,128)(2,1)}, u32[]{:S(2)}) copy-start(bf16[2048,256]{1,0:T(8,128)(2,1)} %param.27) | copy-start | bytes 3145732
  7.2 21.1 %copy-start.3 = (bf16[2,256]{1,0:T(2,128)(2,1)S(1)}, bf16[2,256]{1,0:T(2,128)(2,1)}, u32[]{:S(2)}) copy-start(bf16[2,256]{1,0:T(2,128)(2,1)} %param.24) | copy-start | bytes 3076
  7.2 25.8 %copy-start.5 = (s32[128]{0:T(128)S(1)}, s32[128]{0:T(128)}, u32[]{:S(2)}) copy-start(s32[128]{0:T(128)} %param.25) | copy-start | bytes 1540
  7.2 133.3 %all-gather.2.cloned.1.call-start = ((), (), s32[]{:S(2)}) async-start(), calls=%async_computation | async-start | bytes 2949120 | tf_op jit(solution)/shard_map/all_gather | solution.py:138
  10.5 29.0 %copy-start.2 = (bf16[2,256]{1,0:T(2,128)(2,1)S(1)}, bf16[2,256]{1,0:T(2,128)(2,1)}, u32[]{:S(2)}) copy-start(bf16[2,256]{1,0:T(2,128)(2,1)} %param.22) | copy-start | bytes 3076
  11.6 42.9 %collective-permute-start.1 = (bf16[1024,256]{1,0:T(8,128)(2,1)S(1)}, bf16[1024,256]{1,0:T(8,128)(2,1)}, u32[]{:S(2)}, u32[]{:S(2)}) collective-permute-start(bf16[1024,256]{1,0:T(8,128)(2,1)S(1)} %dynamic-slice_bitcast_fusion.1), channel_id=1, source_target_pairs={{256,0},{264,8},{272,16},{280,24},{288,32},{296,40},{304,48},{312,... | collective-permute-start | bytes 1572872 | tf_op jit(solution)/shard_map/ppermute | solution.py:22
  17.7 38.7 %collective-permute-start.2 = (bf16[256]{0:T(256)(128)(2,1)}, bf16[256]{0:T(256)(128)(2,1)}, u32[]{:S(2)}, u32[]{:S(2)}) collective-permute-start(bf16[256]{0:T(256)(128)(2,1)} %get-tuple-element.10), channel_id=1, source_target_pairs={{256,0},{264,8},{272,16},{280,24},{288,32},{296,40},{304,48},{312,... | collective-permute-start | bytes 1544 | tf_op jit(solution)/shard_map/ppermute | solution.py:22
  21.4 35.8 %collective-permute-start = (bf16[256]{0:T(256)(128)(2,1)}, bf16[256]{0:T(256)(128)(2,1)}, u32[]{:S(2)}, u32[]{:S(2)}) collective-permute-start(bf16[256]{0:T(256)(128)(2,1)} %fusion.35), channel_id=1, source_target_pairs={{256,0},{264,8},{272,16},{280,24},{288,32},{296,40},{304,48},{312,... | collective-permute-start | bytes 1544 | tf_op jit(solution)/shard_map/ppermute | solution.py:22
  25.9 33.0 %collective-permute-start.3 = (bf16[1024,256]{1,0:T(8,128)(2,1)S(1)}, bf16[1024,256]{1,0:T(8,128)(2,1)}, u32[]{:S(2)}, u32[]{:S(2)}) collective-permute-start(bf16[1024,256]{1,0:T(8,128)(2,1)S(1)} %dynamic-slice_bitcast_fusion), channel_id=1, source_target_pairs={{256,0},{264,8},{272,16},{280,24},{288,32},{296,40},{304,48},{312,... | collective-permute-start | bytes 1572872 | tf_op jit(solution)/shard_map/ppermute | solution.py:22
  28.9 31.9 %collective-permute-start.4 = (bf16[256]{0:T(256)(128)(2,1)}, bf16[256]{0:T(256)(128)(2,1)}, u32[]{:S(2)}, u32[]{:S(2)}) collective-permute-start(bf16[256]{0:T(256)(128)(2,1)} %get-tuple-element.12), channel_id=1, source_target_pairs={{256,0},{264,8},{272,16},{280,24},{288,32},{296,40},{304,48},{312,... | collective-permute-start | bytes 1544 | tf_op jit(solution)/shard_map/ppermute | solution.py:22
  46.5 3.0 %copy-start.4 = (f32[2]{0:T(128)S(1)}, f32[2]{0:T(128)}, u32[]{:S(2)}) copy-start(f32[2]{0:T(128)} %multiply_exponential_fusion) | copy-start | bytes 28
  51.6 6.9 %copy-start.1 = (bf16[260,2,128]{2,1,0:T(2,128)(2,1)S(1)}, bf16[260,2,128]{2,1,0:T(2,128)(2,1)}, u32[]{:S(2)}) copy-start(bf16[260,2,128]{2,1,0:T(2,128)(2,1)} %pad_maximum_fusion.2) | copy-start | bytes 399364
  57.2 83.3 %copy-start.8 = (bf16[514,256]{1,0:T(8,128)(2,1)S(1)}, bf16[514,256]{1,0:T(8,128)(2,1)}, u32[]{:S(2)}) copy-start(bf16[514,256]{1,0:T(8,128)(2,1)} %param.29) | copy-start | bytes 789508
  57.2 83.3 %copy-start.9 = (f32[256]{0:T(256)S(1)}, f32[256]{0:T(256)}, u32[]{:S(2)}) copy-start(f32[256]{0:T(256)} %param.28) | copy-start | bytes 3076
  65.0 120.1 %copy-start.6 = (f32[256]{0:T(256)S(1)}, f32[256]{0:T(256)}, u32[]{:S(2)}) copy-start(f32[256]{0:T(256)} %param.31) | copy-start | bytes 3076
  65.0 120.1 %copy-start.7 = (f32[256]{0:T(256)S(1)}, f32[256]{0:T(256)}, u32[]{:S(2)}) copy-start(f32[256]{0:T(256)} %param.30) | copy-start | bytes 3076
Sparse Core Ops, SparseCore 0:
  62.9 77.5 all-gather.1
where the time goes:
time: 194 us; the launch traced here: 193 us
  waiting for transfers between devices  75.5 us (39%)
  blocking collectives  41.6 us (21%)
  between operations  21.3 us (11%)
  local copies, waits for them, and re-layouts  17.8 us (9%)
  starting transfers between devices  15.1 us (8%)
  matrix products  11.9 us (6%)
  other arithmetic  9.62 us (5%)
    all_gather x1, waiting for transfers between devices, on_device(): lax.all_gather(mixed_rows, 'tp', axis=1, tiled=True)  75.5 us
    psum x1, blocking collectives, on_device(): row_var = lax.psum(jnp.sum(centered * centered, axis=1), 'tp') / D  21.7 us
    psum x1, blocking collectives, on_device(): row_mean = lax.psum(row_total, 'tp') / D  19.9 us
    ppermute x5, starting transfers between devices, from_behind(): return lax.ppermute(block, axis, route)  15.1 us
  transfers between devices with their start and end apart: 6, of which 1 were waited for; matrix products, arithmetic and copies ran while one was open for 16% of the time, Pallas kernels for 0%

commit v1 on v0

v1 whole, which is shorter than its diff:
```python
import functools
import math

import jax
import jax.numpy as jnp
from jax import lax
from jax.experimental import pallas as pl
from jax.experimental.pallas import tpu as pltpu
from jax.sharding import PartitionSpec as P

D = 2048
HEADS = 16
HD = 128
SINK = 4
WIN = 256
SPAN = SINK + WIN
ROW_TILE = 16
COPY = 272

LOG2E = math.log2(math.e)
SCALE = LOG2E / math.sqrt(HD)
MASKED = -1e30
EPSILON = 1e-05

F32 = jnp.float32
BF16 = jnp.bfloat16
HIGHEST = lax.Precision.HIGHEST


def dot(a, b, contract, precision=None):
    return lax.dot_general(a, b, (contract, ((), ())), precision=precision, preferred_element_type=F32)


def head_slope(local_heads, head):
    tp = lax.axis_index("tp")
    slope = jnp.float32(LOG2E * 2.0 ** (-8.0 * (head + 1) / HEADS))
    step = 2.0 ** (-8.0 * local_heads / HEADS)
    for k in range(1, HEADS // local_heads):
        slope = jnp.where(tp >= k, slope * step, slope)
    return slope


def decode_kernel(
    moving, cache_len, new_q, new_k, new_v, cache_k, cache_v,
    window_out, stay_out, leave_out, body, sink, sems,
):
    rep = lax.axis_index("rep")
    slots, capacity, width = cache_k.shape
    local_heads = width // HD
    leaving = moving[rep]
    slot_of = (leaving, 1 - leaving)
    copies = []
    offsets, lengths = [], []
    for n, slot in enumerate(slot_of):
        length = cache_len[rep * slots + slot]
        first = length + 1 - WIN
        start = pl.multiple_of(
            jnp.minimum(lax.div(first, ROW_TILE) * ROW_TILE, capacity - COPY), ROW_TILE
        )
        offsets.append(first - start)
        lengths.append(length)
        for kv, cache in enumerate((cache_k, cache_v)):
            copies.append((
                pltpu.make_async_copy(
                    cache.at[slot, pl.ds(start, COPY)], body.at[n, kv], sems.at[n, kv, 0]
                ),
                pltpu.make_async_copy(
                    cache.at[slot, pl.ds(0, ROW_TILE)], sink.at[n, kv], sems.at[n, kv, 1]
                ),
            ))
    for pair in copies:
        for copy in pair:
            copy.start()

    row = lax.broadcasted_iota(jnp.int32, (8, width), 0)
    lane = lax.broadcasted_iota(jnp.int32, (8, width), 1)
    own = row == lax.div(lane, HD)
    head_row = lax.broadcasted_iota(jnp.int32, (8, COPY), 0)
    column = lax.broadcasted_iota(jnp.int32, (8, COPY), 1)
    slopes = jnp.zeros((8, COPY), F32)
    for h in range(local_heads):
        slopes = jnp.where(head_row == h, head_slope(local_heads, h), slopes)

    for n, slot in enumerate(slot_of):
        def newest(ref, slot=slot):
            both = ref[...].astype(F32)
            return jnp.where(slot == 0, both[0:1], both[1:2])

        windows = []
        for kv, new in enumerate((new_k, new_v)):
            for copy in copies[2 * n + kv]:
                copy.wait()
            rolled = pltpu.roll(
                body[n, kv].astype(F32), lax.rem(COPY + SINK - offsets[n], COPY), 0
            )
            top = jnp.where(row < SINK, sink[n, kv].astype(F32)[:8], rolled[:8])
            tail = jnp.where(row == SPAN - 1 - WIN, newest(new), rolled[WIN : WIN + 8])
            window = jnp.concatenate([top, rolled[8:WIN], tail, rolled[WIN + 8 :]], axis=0).astype(BF16)
            if n == 0:
                window_out[0, kv] = window[:SPAN]
            windows.append(window)
        query = jnp.where(own, newest(new_q), 0.0).astype(BF16)
        scores = dot(query, windows[0], ((1,), (1,))) * SCALE
        distance = jnp.where(column < SINK, lengths[n] - column, SPAN - 1 - column).astype(F32)
        scores = jnp.where(column < SPAN, scores - slopes * distance, MASKED)
        terms = jnp.exp2(scores - jnp.max(scores, axis=1, keepdims=True))
        weights = (terms / jnp.sum(terms, axis=1, keepdims=True)).astype(BF16)
        mixed = dot(weights, windows[1], ((1,), (0,)))
        mixed = jnp.sum(jnp.where(own, mixed, 0.0), axis=0, keepdims=True)
        (leave_out, stay_out)[n][...] = mixed.astype(BF16)


def decode(moving, cache_len, new_q, new_k, new_v, cache_k, cache_v):
    slots, _, width = cache_k.shape
    smem = pl.BlockSpec(memory_space=pltpu.SMEM)
    vmem = pl.BlockSpec(memory_space=pltpu.VMEM)
    hbm = pl.BlockSpec(memory_space=pl.ANY)
    return pl.pallas_call(
        decode_kernel,
        name="decode",
        out_shape=(
            jax.ShapeDtypeStruct((1, 2, SPAN, width), BF16),
            jax.ShapeDtypeStruct((1, width), BF16),
            jax.ShapeDtypeStruct((1, width), BF16),
        ),
        in_specs=[smem, smem, vmem, vmem, vmem, hbm, hbm],
        out_specs=(vmem, vmem, vmem),
        scratch_shapes=[
            pltpu.VMEM((2, 2, COPY, width), BF16),
            pltpu.VMEM((2, 2, ROW_TILE, width), BF16),
            pltpu.SemaphoreType.DMA((2, 2, 2)),
        ],
    )(moving, cache_len, new_q, new_k, new_v, cache_k, cache_v)


def prompt_kernel(length_ref, q_ref, k_ref, v_ref, out_ref, *, block):
    rows, width = q_ref.shape
    length = length_ref[0]
    for b in range(rows // block):
        keys = (b + 1) * block
        query_at = lax.broadcasted_iota(jnp.int32, (block, keys), 0) + b * block
        key_at = lax.broadcasted_iota(jnp.int32, (block, keys), 1)
        allowed = (key_at <= query_at) & (key_at < length)
        distance = (query_at - key_at).astype(F32)
        for h in range(width // HD):
            cols = slice(h * HD, (h + 1) * HD)
            scores = dot(
                q_ref[b * block : keys, cols], k_ref[:keys, cols], ((1,), (1,))
            ) * SCALE
            scores = jnp.where(
                allowed, scores - head_slope(width // HD, h) * distance, MASKED
            )
            terms = jnp.exp2(scores - jnp.max(scores, axis=1, keepdims=True))
            weights = (terms / jnp.sum(terms, axis=1, keepdims=True)).astype(BF16)
            out_ref[b * block : keys, cols] = dot(
                weights, v_ref[:keys, cols], ((1,), (0,))
            ).astype(BF16)


def prompt(length, q, k, v):
    vmem = pl.BlockSpec(memory_space=pltpu.VMEM)
    return pl.pallas_call(
        functools.partial(prompt_kernel, block=256),
        name="prompt",
        out_shape=jax.ShapeDtypeStruct(q.shape, BF16),
        in_specs=[pl.BlockSpec(memory_space=pltpu.SMEM), vmem, vmem, vmem],
        out_specs=vmem,
    )(length, q, k, v)


def project_kernel(x_ref, w_ref, bias_ref, residual_ref, hidden_ref, stream_ref, stats_ref):
    source = pl.program_id(0)
    part = dot(x_ref[0], w_ref[...], ((1,), (0,)))

    @pl.when(source == 0)
    def _():
        stream_ref[...] = part

    @pl.when(source > 0)
    def _():
        stream_ref[...] += part

    @pl.when(source == pl.num_programs(0) - 1)
    def _():
        stream = stream_ref[...] + bias_ref[...] + residual_ref[...].astype(F32)
        stream_ref[...] = stream
        hidden_ref[...] = stream.astype(BF16)
        width = stream.shape[1]
        mean = jnp.sum(stream, axis=1, keepdims=True) * (1.0 / width)
        centered = stream - mean
        spread = jnp.sum(centered * centered, axis=1, keepdims=True)
        lane = lax.broadcasted_iota(jnp.int32, (stream.shape[0], HD), 1)
        table = jnp.where(lane == 0, mean, jnp.where(lane == 1, spread, 0.0))
        pick = lax.broadcasted_iota(jnp.int32, (8, HD), 0) == lax.broadcasted_iota(jnp.int32, (8, HD), 1)
        stats_ref[...] = dot(pick.astype(F32), table, ((1,), (1,)), HIGHEST)[:2]


def project(gathered, weight, bias, residual):
    sources, rows, width = gathered.shape
    whole = lambda s: (0, 0)
    return pl.pallas_call(
        project_kernel,
        name="project",
        grid=(sources,),
        out_shape=(
            jax.ShapeDtypeStruct((rows, width), BF16),
            jax.ShapeDtypeStruct((rows, width), F32),
            jax.ShapeDtypeStruct((2, rows), F32),
        ),
        in_specs=[
            pl.BlockSpec((1, rows, width), lambda s: (s, 0, 0)),
            pl.BlockSpec((width, width), lambda s: (s, 0)),
            pl.BlockSpec((1, width), whole),
            pl.BlockSpec((rows, width), whole),
        ],
        out_specs=(
            pl.BlockSpec((rows, width), whole),
            pl.BlockSpec((rows, width), whole),
            pl.BlockSpec((2, rows), whole),
        ),
    )(gathered, weight, bias, residual)


def norm_kernel(stats_ref, stream_ref, gain_ref, shift_ref, out_ref):
    parts = stats_ref.shape[0]
    rows, width = stream_ref.shape
    means = stats_ref[:, 0, :]
    mean = jnp.sum(means, axis=0, keepdims=True) * (1.0 / parts)
    apart = means - mean
    spread = jnp.sum(stats_ref[:, 1, :] + width * (apart * apart), axis=0, keepdims=True)
    scale = lax.rsqrt(spread * (1.0 / (parts * width)) + EPSILON)
    row = lax.broadcasted_iota(jnp.int32, (8, rows), 0)
    table = jnp.where(row == 0, mean, jnp.where(row == 1, scale, 0.0))
    at = lax.broadcasted_iota(jnp.int32, (8, width), 0)
    mean_all = dot(table, (at == 0).astype(F32), ((0,), (0,)), HIGHEST)
    scale_all = dot(table, (at == 1).astype(F32), ((0,), (0,)), HIGHEST)
    out_ref[...] = (
        (stream_ref[...] - mean_all) * scale_all * gain_ref[...] + shift_ref[...]
    ).astype(BF16)


def norm(stats, stream, gain, shift):
    vmem = pl.BlockSpec(memory_space=pltpu.VMEM)
    return pl.pallas_call(
        norm_kernel,
        name="norm",
        out_shape=jax.ShapeDtypeStruct(stream.shape, BF16),
        in_specs=[vmem] * 4,
        out_specs=vmem,
    )(stats, stream, gain, shift)


def to_partner(block):
    count = lax.axis_size("rep")
    return lax.ppermute(block, "rep", [(i, (i + count // 2) % count) for i in range(count)])


def to_all(block):
    count = lax.axis_size("tp")
    return lax.all_to_all(jnp.broadcast_to(block[None], (count, *block.shape)), "tp", 0, 0)


def on_device(
    prompt_q, prompt_k, prompt_v, prompt_len, cache_keys, cache_values, new_q, new_k, new_v,
    cache_len, moving, out_weight, out_bias, residual, ln_gain, ln_shift,
):
    window, stay_row, leave_row = decode(
        moving, cache_len, new_q, new_k, new_v, cache_keys, cache_values
    )
    come_row = to_partner(leave_row)
    moved_window = to_partner(window)
    prompt_mix = prompt(prompt_len, prompt_q, prompt_k, prompt_v)
    mixed_rows = jnp.concatenate([prompt_mix, stay_row, come_row], axis=0)
    hidden_out, stream, stats = project(
        to_all(mixed_rows), out_weight, out_bias[None], residual
    )
    normed = norm(to_all(stats), stream, ln_gain[None], ln_shift[None])
    return (hidden_out, normed, moved_window)


def solution(mesh):
    in_specs = (
        P("rep", "tp"), P("rep", "tp"), P("rep", "tp"), P("rep"),
        P("rep", None, "tp"), P("rep", None, "tp"),
        P("rep", "tp"), P("rep", "tp"), P("rep", "tp"),
        P(), P(), P(None, "tp"), P("tp"), P("rep", "tp"), P("tp"), P("tp"),
    )
    out_specs = (P("rep", "tp"), P("rep", "tp"), P("rep", None, None, "tp"))
    return jax.shard_map(
        on_device, mesh=mesh, in_specs=in_specs, out_specs=out_specs, check_vma=False
    )
```

time: 194 us -> 76.2 us (0.39)
  the two profiles are of different devices: /device:TPU:32 before, /device:TPU:480 now
where the time goes in v1:
time: 76.2 us; the launch traced here: 75.7 us
  waiting for transfers between devices  34.9 us (46%)
  Pallas kernels  17.1 us (22%)
  starting transfers between devices  15.6 us (20%)
  local copies, waits for them, and re-layouts  5.67 us (7%)
  between operations  1.33 us (2%)
  other arithmetic  0.99 us (1%)
    all_to_all x2, waiting for transfers between devices, to_all(): lax.all_to_all(jnp.broadcast_to(block[None], (count, *block.shape)), 'tp'...  34.9 us
    all_to_all x2, starting transfers between devices, to_all(): lax.all_to_all(jnp.broadcast_to(block[None], (count, *block.shape)), 'tp'...  10.1 us
    pallas_call x1, Pallas kernels, project(): pl.pallas_call(project_kernel, name='project', grid=(sources,), out_shape...  7.07 us
    ppermute x2, starting transfers between devices, to_partner(): lax.ppermute(block, 'rep', [(i, (i + count // 2) % count) for i in range(...  5.53 us
    pallas_call x1, Pallas kernels, prompt(): pl.pallas_call(functools.partial(prompt_kernel, block=256), name='prompt'...  3.64 us
    pallas_call x1, Pallas kernels, decode(): pl.pallas_call(decode_kernel, name='decode', out_shape=(jax.ShapeDtypeStr...  3.58 us
    unnamed x7, local copies, waits for them, and re-layouts  2.87 us
    pallas_call x1, Pallas kernels, norm(): pl.pallas_call(norm_kernel, name='norm', out_shape=jax.ShapeDtypeStruct(s...  2.83 us
  transfers between devices with their start and end apart: 4, of which 2 were waited for; matrix products, arithmetic and copies ran while one was open for 3% of the time, Pallas kernels for 14%

profile of v1, /device:TPU:480, one launch (start us, length us, event | category | flops | bytes accessed | tf_op | source)
XLA Modules:
  0.0 75.7 jit_solution(11176688428689158850)
XLA Ops:
  0.6 3.6 %decode.1 = (bf16[1,2,260,256]{3,2,1,0:T(8,128)(2,1)}, bf16[1,256]{1,0:T(2,128)(2,1)}, bf16[1,256]{1,0:T(2,128)(2,1)}) custom-call(s32[64]{0:T(128)} %moving.1, s32[128]{0:T(128)} %cache_len.1, bf16[2,256]{1,0:T(2,128)(2,1)} %new_q.1, bf16[2,256]{1,0:T(2,128)(2,1)} %new_k.1, bf16[2,256]{1,0:T(2,128)(2,1)} %new_v.1, bf16[2,1024,256]{2,1,0:T(8,128)(2,1)} %cache_k.1, ...), custom_call_target="tpu_custom_call" | custom-call | tf_op jit(solution)/shard_map/decode/pallas_call | solution.py:118
  4.2 3.4 %collective-permute-start = (bf16[1,256]{1,0:T(2,128)(2,1)}, bf16[1,256]{1,0:T(2,128)(2,1)S(1)}, u32[]{:S(2)}, u32[]{:S(2)}) collective-permute-start(bf16[1,256]{1,0:T(2,128)(2,1)} %get-tuple-element.10), channel_id=1, source_target_pairs={{0,256},{8,264},{16,272},{24,280},{32,288},{40,296},{48,304},{56,3... | collective-permute-start | bytes 1544 | tf_op jit(solution)/shard_map/ppermute | solution.py:255
  8.3 3.6 %prompt.1 = bf16[512,256]{1,0:T(8,128)(2,1)} custom-call(s32[1]{0:T(128)S(6)} %copy.20.length_ref, bf16[512,256]{1,0:T(8,128)(2,1)} %q_ref.1, bf16[512,256]{1,0:T(8,128)(2,1)} %k_ref.1, bf16[512,256]{1,0:T(8,128)(2,1)} %v_ref.1), custom_call_target="tpu_custom_call" | custom-call | tf_op jit(solution)/shard_map/prompt/pallas_call | solution.py:162
  11.9 0.0 collective-permute-done
  11.9 1.0 %pad_maximum_fusion = bf16[514,256]{1,0:T(8,128)(2,1)S(1)} fusion(bf16[1,256]{1,0:T(2,128)(2,1)S(1)} %collective-permute-done, bf16[1,256]{1,0:T(2,128)(2,1)} %get-tuple-element.9, bf16[512,256]{1,0:T(8,128)(2,1)} %prompt.1), kind=kLoop, calls=%fused_computation | loop fusion | flops 789504 | bytes 526336 | tf_op jit(solution)/shard_map/concatenate | solution.py:273
  12.9 1.5 %broadcast_in_dim.10 = bf16[8,514,256]{2,1,0:T(8,128)(2,1)} broadcast(bf16[514,256]{1,0:T(8,128)(2,1)S(1)} %pad_maximum_fusion), dimensions={1,2} | broadcast | bytes 2368512 | tf_op jit(solution)/shard_map/broadcast_in_dim | solution.py:260
  14.4 0.0 copy-start.2
  14.4 6.8 %all-to-all-start = ((bf16[8,514,256]{2,1,0:T(8,128)(2,1)}), bf16[8,514,256]{2,1,0:T(8,128)(2,1)S(1)}, u32[]{:S(2)}, u32[]{:S(2)}) async-start(bf16[8,514,256]{2,1,0:T(8,128)(2,1)} %broadcast_in_dim.10), calls=%async_computation | async-start | bytes 4259840 | tf_op jit(solution)/shard_map/all_to_all | solution.py:260
  21.2 0.0 copy-done.2
  21.2 2.1 %collective-permute-start.1 = (bf16[1,2,260,256]{3,2,1,0:T(8,128)(2,1)S(1)}, bf16[1,2,260,256]{3,2,1,0:T(8,128)(2,1)S(1)}, u32[]{:S(2)}, u32[]{:S(2)}) collective-permute-start(bf16[1,2,260,256]{3,2,1,0:T(8,128)(2,1)S(1)} %copy-done.2), channel_id=1, source_target_pairs={{0,256},{8,264},{16,272},{24,280},{32,288},{40,296},{48,304},{56,3... | collective-permute-start | bytes 798728 | tf_op jit(solution)/shard_map/ppermute | solution.py:255
  23.3 28.1 %all-to-all-done.x_ref = bf16[8,514,256]{2,1,0:T(8,128)(2,1)S(1)} async-done(((bf16[8,514,256]{2,1,0:T(8,128)(2,1)}), bf16[8,514,256]{2,1,0:T(8,128)(2,1)S(1)}, u32[]{:S(2)}, u32[]{:S(2)}) %all-to-all-start) | async-done | bytes 2105376 | tf_op jit(solution)/shard_map/all_to_all | solution.py:260
  51.4 0.0 copy-start
  51.4 1.3 %copy-done = bf16[8,514,256]{2,1,0:T(8,128)(2,1)} copy-done((bf16[8,514,256]{2,1,0:T(8,128)(2,1)}, bf16[8,514,256]{2,1,0:T(8,128)(2,1)S(1)}, u32[]{:S(2)}) %copy-start) | copy-done | bytes 2105368
  52.8 7.1 %project.1 = (bf16[514,256]{1,0:T(8,128)(2,1)}, f32[514,256]{1,0:T(8,128)}, f32[2,514]{1,0:T(2,128)}) custom-call(bf16[8,514,256]{2,1,0:T(8,128)(2,1)} %copy-done, bf16[2048,256]{1,0:T(8,128)(2,1)} %w_ref.1, f32[1,256]{1,0:T(1,128)} %bitcast.3, bf16[514,256]{1,0:T(8,128)(2,1)} %residual_ref.1), custom_call_target="tpu_custom_call" | custom-call | tf_op jit(solution)/shard_map/project/pallas_call | solution.py:201
  59.8 1.3 %broadcast_in_dim.23 = f32[8,2,514]{2,1,0:T(2,128)} broadcast(f32[2,514]{1,0:T(2,128)} %get-tuple-element.12), dimensions={1,2} | broadcast | bytes 37008 | tf_op jit(solution)/shard_map/broadcast_in_dim | solution.py:260
  61.2 3.3 %all-to-all-start.1 = ((f32[8,2,514]{2,1,0:T(2,128)}), f32[8,2,514]{2,1,0:T(2,128)S(1)}, u32[]{:S(2)}, u32[]{:S(2)}) async-start(f32[8,2,514]{2,1,0:T(2,128)} %broadcast_in_dim.23), calls=%async_computation.1 | async-start | bytes 81920 | tf_op jit(solution)/shard_map/all_to_all | solution.py:260
  64.5 0.0 collective-permute-done.1
  64.5 0.9 %copy.19 = bf16[1,2,260,256]{3,1,2,0:T(2,128)(2,1)} copy(bf16[1,2,260,256]{3,2,1,0:T(8,128)(2,1)S(1)} %collective-permute-done.1) | data formatting | bytes 532480
  65.4 6.8 %all-to-all-done.1.stats_ref = f32[8,2,514]{2,1,0:T(2,128)S(1)} async-done(((f32[8,2,514]{2,1,0:T(2,128)}), f32[8,2,514]{2,1,0:T(2,128)S(1)}, u32[]{:S(2)}, u32[]{:S(2)}) %all-to-all-start.1) | async-done | bytes 32928 | tf_op jit(solution)/shard_map/all_to_all | solution.py:260
  72.2 0.0 copy-start.1
  72.2 0.6 copy-done.1
  72.8 2.8 %norm.1 = bf16[514,256]{1,0:T(8,128)(2,1)} custom-call(f32[8,2,514]{2,1,0:T(2,128)} %copy-done.1, f32[514,256]{1,0:T(8,128)} %get-tuple-element.13.stream_ref, f32[1,256]{1,0:T(1,128)} %bitcast.4, f32[1,256]{1,0:T(1,128)} %bitcast.5), custom_call_target="tpu_custom_call" | custom-call | tf_op jit(solution)/shard_map/norm/pallas_call | solution.py:244
Async XLA Ops:
  4.2 7.7 %collective-permute-start = (bf16[1,256]{1,0:T(2,128)(2,1)}, bf16[1,256]{1,0:T(2,128)(2,1)S(1)}, u32[]{:S(2)}, u32[]{:S(2)}) collective-permute-start(bf16[1,256]{1,0:T(2,128)(2,1)} %get-tuple-element.10), channel_id=1, source_target_pairs={{0,256},{8,264},{16,272},{24,280},{32,288},{40,296},{48,304},{56,3... | collective-permute-start | bytes 1544 | tf_op jit(solution)/shard_map/ppermute | solution.py:255
  14.4 6.8 %copy-start.2 = (bf16[1,2,260,256]{3,2,1,0:T(8,128)(2,1)S(1)}, bf16[1,2,260,256]{3,2,1,0:T(8,128)(2,1)}, u32[]{:S(2)}) copy-start(bf16[1,2,260,256]{3,2,1,0:T(8,128)(2,1)} %get-tuple-element.14) | copy-start | bytes 798724
  14.4 37.0 %all-to-all-start = ((bf16[8,514,256]{2,1,0:T(8,128)(2,1)}), bf16[8,514,256]{2,1,0:T(8,128)(2,1)S(1)}, u32[]{:S(2)}, u32[]{:S(2)}) async-start(bf16[8,514,256]{2,1,0:T(8,128)(2,1)} %broadcast_in_dim.10), calls=%async_computation | async-start | bytes 4259840 | tf_op jit(solution)/shard_map/all_to_all | solution.py:260
  21.2 43.3 %collective-permute-start.1 = (bf16[1,2,260,256]{3,2,1,0:T(8,128)(2,1)S(1)}, bf16[1,2,260,256]{3,2,1,0:T(8,128)(2,1)S(1)}, u32[]{:S(2)}, u32[]{:S(2)}) collective-permute-start(bf16[1,2,260,256]{3,2,1,0:T(8,128)(2,1)S(1)} %copy-done.2), channel_id=1, source_target_pairs={{0,256},{8,264},{16,272},{24,280},{32,288},{40,296},{48,304},{56,3... | collective-permute-start | bytes 798728 | tf_op jit(solution)/shard_map/ppermute | solution.py:255
  51.4 1.3 %copy-start = (bf16[8,514,256]{2,1,0:T(8,128)(2,1)}, bf16[8,514,256]{2,1,0:T(8,128)(2,1)S(1)}, u32[]{:S(2)}) copy-start(bf16[8,514,256]{2,1,0:T(8,128)(2,1)S(1)} %all-to-all-done.x_ref) | copy-start | bytes 6316036
  61.2 11.1 %all-to-all-start.1 = ((f32[8,2,514]{2,1,0:T(2,128)}), f32[8,2,514]{2,1,0:T(2,128)S(1)}, u32[]{:S(2)}, u32[]{:S(2)}) async-start(f32[8,2,514]{2,1,0:T(2,128)} %broadcast_in_dim.23), calls=%async_computation.1 | async-start | bytes 81920 | tf_op jit(solution)/shard_map/all_to_all | solution.py:260
  72.2 0.6 copy-start.1

commit v2 on v1

v2 whole, which is shorter than its diff:
```python
import functools
import math

import jax
import jax.numpy as jnp
from jax import lax
from jax.experimental import pallas as pl
from jax.experimental.pallas import tpu as pltpu
from jax.sharding import PartitionSpec as P

D = 2048
HEADS = 16
HD = 128
SINK = 4
WIN = 256
SPAN = SINK + WIN
ROW_TILE = 16
COPY = 272

LOG2E = math.log2(math.e)
SCALE = LOG2E / math.sqrt(HD)
MASKED = -1e30
EPSILON = 1e-05
BLOCK = 128
ROOM = 16 * 2**20

F32 = jnp.float32
BF16 = jnp.bfloat16
HIGHEST = lax.Precision.HIGHEST

SMEM = pl.BlockSpec(memory_space=pltpu.SMEM)
VMEM = pl.BlockSpec(memory_space=pltpu.VMEM)
HBM = pl.BlockSpec(memory_space=pl.ANY)


def kept(shape, dtype):
    return pltpu.VMEM(shape, dtype)


def placed(shape, dtype):
    return pltpu.HBM(shape, dtype)


def near(array):
    return pltpu.with_memory_space_constraint(array, pltpu.VMEM)


def far(array):
    return pltpu.with_memory_space_constraint(array, pltpu.HBM)


def dot(a, b, contract, precision=None):
    return lax.dot_general(a, b, (contract, ((), ())), precision=precision, preferred_element_type=F32)


def head_slope(local_heads, head):
    tp = lax.axis_index("tp")
    slope = jnp.float32(LOG2E * 2.0 ** (-8.0 * (head + 1) / HEADS))
    step = 2.0 ** (-8.0 * local_heads / HEADS)
    for k in range(1, HEADS // local_heads):
        slope = jnp.where(tp >= k, slope * step, slope)
    return slope


def decode_kernel(
    moving_hbm, cache_len_hbm, new_q_hbm, new_k_hbm, new_v_hbm, cache_k, cache_v,
    window_out, stay_out, leave_out, moving, cache_len, new_q, new_k, new_v, body, sink, sems, small_sems,
):
    small = [
        pltpu.make_async_copy(source, target, small_sems.at[i])
        for i, (source, target) in enumerate((
            (moving_hbm, moving), (cache_len_hbm, cache_len),
            (new_q_hbm, new_q), (new_k_hbm, new_k), (new_v_hbm, new_v),
        ))
    ]
    for copy in small:
        copy.start()
    small[0].wait()
    small[1].wait()
    rep = lax.axis_index("rep")
    slots, capacity, width = cache_k.shape
    local_heads = width // HD
    leaving = moving[rep]
    slot_of = (leaving, 1 - leaving)
    copies = []
    offsets, lengths = [], []
    for n, slot in enumerate(slot_of):
        length = cache_len[rep * slots + slot]
        first = length + 1 - WIN
        start = pl.multiple_of(
            jnp.minimum(lax.div(first, ROW_TILE) * ROW_TILE, capacity - COPY), ROW_TILE
        )
        offsets.append(first - start)
        lengths.append(length)
        for kv, cache in enumerate((cache_k, cache_v)):
            copies.append((
                pltpu.make_async_copy(
                    cache.at[slot, pl.ds(start, COPY)], body.at[n, kv], sems.at[n, kv, 0]
                ),
                pltpu.make_async_copy(
                    cache.at[slot, pl.ds(0, ROW_TILE)], sink.at[n, kv], sems.at[n, kv, 1]
                ),
            ))
    for pair in copies:
        for copy in pair:
            copy.start()

    for copy in small[2:]:
        copy.wait()

    row = lax.broadcasted_iota(jnp.int32, (8, width), 0)
    lane = lax.broadcasted_iota(jnp.int32, (8, width), 1)
    own = row == lax.div(lane, HD)
    head_row = lax.broadcasted_iota(jnp.int32, (8, COPY), 0)
    column = lax.broadcasted_iota(jnp.int32, (8, COPY), 1)
    slopes = jnp.zeros((8, COPY), F32)
    for h in range(local_heads):
        slopes = jnp.where(head_row == h, head_slope(local_heads, h), slopes)

    for n, slot in enumerate(slot_of):
        def newest(ref, slot=slot):
            both = ref[...].astype(F32)
            return jnp.where(slot == 0, both[0:1], both[1:2])

        windows = []
        for kv, new in enumerate((new_k, new_v)):
            for copy in copies[2 * n + kv]:
                copy.wait()
            rolled = pltpu.roll(
                body[n, kv].astype(F32), lax.rem(COPY + SINK - offsets[n], COPY), 0
            )
            top = jnp.where(row < SINK, sink[n, kv].astype(F32)[:8], rolled[:8])
            tail = jnp.where(row == SPAN - 1 - WIN, newest(new), rolled[WIN : WIN + 8])
            window = jnp.concatenate([top, rolled[8:WIN], tail, rolled[WIN + 8 :]], axis=0).astype(BF16)
            if n == 0:
                window_out[0, kv] = window[:SPAN]
            windows.append(window)
        query = jnp.where(own, newest(new_q), 0.0).astype(BF16)
        scores = dot(query, windows[0], ((1,), (1,))) * SCALE
        distance = jnp.where(column < SINK, lengths[n] - column, SPAN - 1 - column).astype(F32)
        scores = jnp.where(column < SPAN, scores - slopes * distance, MASKED)
        terms = jnp.exp2(scores - jnp.max(scores, axis=1, keepdims=True))
        weights = (terms / jnp.sum(terms, axis=1, keepdims=True)).astype(BF16)
        mixed = dot(weights, windows[1], ((1,), (0,)))
        mixed = jnp.sum(jnp.where(own, mixed, 0.0), axis=0, keepdims=True)
        (leave_out, stay_out)[n][...] = mixed.astype(BF16)


def decode(moving, cache_len, new_q, new_k, new_v, cache_k, cache_v):
    width = cache_k.shape[2]
    return pl.pallas_call(
        decode_kernel,
        name="decode",
        compiler_params=pltpu.CompilerParams(vmem_limit_bytes=ROOM),
        out_shape=(
            jax.ShapeDtypeStruct((1, 2, SPAN, width), BF16),
            jax.ShapeDtypeStruct((1, width), BF16),
            jax.ShapeDtypeStruct((1, width), BF16),
        ),
        in_specs=[HBM] * 7,
        out_specs=(VMEM, VMEM, VMEM),
        scratch_shapes=[
            pltpu.SMEM(moving.shape, jnp.int32),
            pltpu.SMEM(cache_len.shape, jnp.int32),
            *[pltpu.VMEM(new_q.shape, BF16)] * 3,
            pltpu.VMEM((2, 2, COPY, width), BF16),
            pltpu.VMEM((2, 2, ROW_TILE, width), BF16),
            pltpu.SemaphoreType.DMA((2, 2, 2)),
            pltpu.SemaphoreType.DMA((5,)),
        ],
    )(*map(far, (moving, cache_len, new_q, new_k, new_v, cache_k, cache_v)))


def prompt_kernel(
    length_ref, q_ref, k_ref, v_ref, stay_ref, come_ref, out_hbm, out_ref, sems, *, block,
):
    rows, width = q_ref.shape
    row = lax.broadcasted_iota(jnp.int32, (8, width), 0)
    served = jnp.where(row == 0, stay_ref[...].astype(F32), jnp.where(row == 1, come_ref[...].astype(F32), 0.0))
    out_ref[rows:] = served.astype(BF16)
    length = length_ref[0]
    copies = []
    for step, first in enumerate(range(0, rows, block)):
        keys = first + block
        query_at = lax.broadcasted_iota(jnp.int32, (block, keys), 0) + first
        key_at = lax.broadcasted_iota(jnp.int32, (block, keys), 1)
        allowed = (key_at <= query_at) & (key_at < length)
        distance = (query_at - key_at).astype(F32)
        for h in range(width // HD):
            cols = slice(h * HD, (h + 1) * HD)
            scores = dot(q_ref[first:keys, cols], k_ref[:keys, cols], ((1,), (1,))) * SCALE
            scores = jnp.where(allowed, scores - head_slope(width // HD, h) * distance, MASKED)
            terms = jnp.exp2(scores - jnp.max(scores, axis=1, keepdims=True))
            weights = (terms / jnp.sum(terms, axis=1, keepdims=True)).astype(BF16)
            out_ref[first:keys, cols] = dot(weights, v_ref[:keys, cols], ((1,), (0,))).astype(BF16)
        done = slice(first, keys if keys < rows else rows + 8)
        for member in range(out_hbm.shape[0]):
            copy = pltpu.make_async_copy(out_ref.at[done], out_hbm.at[member, done], sems.at[step, member])
            copy.start()
            copies.append(copy)
    for copy in copies:
        copy.wait()


def prompt(length, q, k, v, stay_row, come_row, members):
    rows, width = q.shape
    block = 256
    return pl.pallas_call(
        functools.partial(prompt_kernel, block=block),
        name="prompt",
        compiler_params=pltpu.CompilerParams(vmem_limit_bytes=ROOM),
        out_shape=placed((members, rows + 8, width), BF16),
        in_specs=[SMEM, VMEM, VMEM, VMEM, VMEM, VMEM],
        out_specs=HBM,
        scratch_shapes=[
            pltpu.VMEM((rows + 8, width), BF16),
            pltpu.SemaphoreType.DMA((rows // block, members)),
        ],
    )(length, near(q), near(k), near(v), stay_row, come_row)


def project_kernel(x_ref, w_ref, bias_ref, residual_hbm, hidden_ref, stream_hbm, stats_ref, residual_ref, sum_ref, sem):
    copy = pltpu.make_async_copy(residual_hbm, residual_ref, sem)
    copy.start()
    sources, _, width = x_ref.shape
    rows = sum_ref.shape[0]
    blocks = [slice(start, min(start + BLOCK, rows)) for start in range(0, rows, BLOCK)]
    for at in blocks:
        sum_ref[at] = sum(
            dot(x_ref[s, at], w_ref[s * width : (s + 1) * width], ((1,), (0,))) for s in range(sources)
        )
    copy.wait()
    for at in blocks:
        size = at.stop - at.start
        stream = sum_ref[at] + bias_ref[...] + residual_ref[at].astype(F32)
        sum_ref[at] = stream
        hidden_ref[at] = stream.astype(BF16)
        mean = jnp.sum(stream, axis=1, keepdims=True) * (1.0 / width)
        centered = stream - mean
        spread = jnp.sum(centered * centered, axis=1, keepdims=True)
        lane = lax.broadcasted_iota(jnp.int32, (size, HD), 1)
        table = jnp.where(lane == 0, mean, jnp.where(lane == 1, spread, 0.0))
        stats = table.T[:2]
        for copy in range(stats_ref.shape[0]):
            stats_ref[copy, :, at] = stats
    out = pltpu.make_async_copy(sum_ref, stream_hbm, sem)
    out.start()
    out.wait()


def project(gathered, weight, bias, residual):
    sources = gathered.shape[0]
    rows, width = residual.shape
    return pl.pallas_call(
        project_kernel,
        name="project",
        compiler_params=pltpu.CompilerParams(vmem_limit_bytes=ROOM),
        out_shape=(
            kept((rows, width), BF16),
            placed((rows, width), F32),
            placed((sources, 2, rows), F32),
        ),
        in_specs=[VMEM, VMEM, VMEM, HBM],
        out_specs=(VMEM, HBM, VMEM),
        scratch_shapes=[
            pltpu.VMEM((rows, width), BF16),
            pltpu.VMEM((rows, width), F32),
            pltpu.SemaphoreType.DMA,
        ],
    )(near(gathered), near(weight), bias, far(residual))


def norm_kernel(stats_ref, stream_hbm, gain_ref, shift_ref, out_ref, stream_ref, sem):
    copy = pltpu.make_async_copy(stream_hbm, stream_ref, sem)
    copy.start()
    parts = stats_ref.shape[0]
    rows, width = stream_ref.shape
    means = stats_ref[:, 0, :]
    mean = jnp.sum(means, axis=0, keepdims=True) * (1.0 / parts)
    apart = means - mean
    spread = jnp.sum(stats_ref[:, 1, :] + width * (apart * apart), axis=0, keepdims=True)
    scale = lax.rsqrt(spread * (1.0 / (parts * width)) + EPSILON)
    row = lax.broadcasted_iota(jnp.int32, (8, rows), 0)
    table = jnp.where(row == 0, mean, jnp.where(row == 1, scale, 0.0))
    copy.wait()
    for start in range(0, rows, BLOCK):
        at = slice(start, min(start + BLOCK, rows))
        columns = table[:, at].T
        out_ref[at] = (
            (stream_ref[at] - columns[:, 0:1]) * columns[:, 1:2] * gain_ref[...] + shift_ref[...]
        ).astype(BF16)


def norm(stats, stream, gain, shift):
    return pl.pallas_call(
        norm_kernel,
        name="norm",
        compiler_params=pltpu.CompilerParams(vmem_limit_bytes=ROOM),
        out_shape=jax.ShapeDtypeStruct(stream.shape, BF16),
        in_specs=[VMEM, HBM, VMEM, VMEM],
        out_specs=VMEM,
        scratch_shapes=[pltpu.VMEM(stream.shape, F32), pltpu.SemaphoreType.DMA],
    )(near(stats), far(stream), gain, shift)


def to_partner(block):
    count = lax.axis_size("rep")
    return lax.ppermute(block, "rep", [(i, (i + count // 2) % count) for i in range(count)])


def exchange(blocks):
    return lax.all_to_all(blocks, "tp", 0, 0)


def after(values, other):
    return lax.optimization_barrier((values, other))[0]


def on_device(
    prompt_q, prompt_k, prompt_v, prompt_len, cache_keys, cache_values, new_q, new_k, new_v,
    cache_len, moving, out_weight, out_bias, residual, ln_gain, ln_shift,
):
    window, stay_row, leave_row = decode(
        moving, cache_len, new_q, new_k, new_v, cache_keys, cache_values
    )
    come_row = to_partner(leave_row)
    window, leave_row = lax.optimization_barrier((window, leave_row))
    moved_window = to_partner(window)
    mixed = prompt(
        prompt_len, prompt_q, prompt_k, prompt_v, stay_row, come_row, lax.axis_size("tp")
    )
    hidden_out, stream, stats = project(exchange(mixed), out_weight, out_bias[None], residual)
    normed = norm(exchange(stats), stream, ln_gain[None], ln_shift[None])
    return (hidden_out, normed, moved_window)


def solution(mesh):
    in_specs = (
        P("rep", "tp"), P("rep", "tp"), P("rep", "tp"), P("rep"),
        P("rep", None, "tp"), P("rep", None, "tp"),
        P("rep", "tp"), P("rep", "tp"), P("rep", "tp"),
        P(), P(), P(None, "tp"), P("tp"), P("rep", "tp"), P("tp"), P("tp"),
    )
    out_specs = (P("rep", "tp"), P("rep", "tp"), P("rep", None, None, "tp"))
    return jax.shard_map(
        on_device, mesh=mesh, in_specs=in_specs, out_specs=out_specs, check_vma=False
    )
```

time: 76.2 us -> 66.7 us (0.88)
  Pallas kernels: 17.1 us -> 11.6 us
  local copies, waits for them, and re-layouts: 5.67 us -> 2.6 us
  other arithmetic: 0.99 us -> 0 us
    pallas_call x4, Pallas kernels: 17.1 us -> 11.6 us  [the longest x1 3.29 us: decode(): pl.pallas_call(decode_kernel, name='decode', compiler_params=pltpu.Compil...]
    broadcast_in_dim x2 -> x0, local copies, waits for them, and re-layouts: 2.8 us -> none  [to_all(): jnp.broadcast_to(block[None], (count, *block.shape))]
    all_to_all x2, waiting for transfers between devices: 34.9 us -> 32.9 us  [exchange(): return lax.all_to_all(blocks, 'tp', 0, 0)]
    ppermute x2, waiting for transfers between devices: 0.01 us -> 1.41 us  [to_partner(): lax.ppermute(block, 'rep', [(i, (i + count // 2) % count) for i in range(...]
    concatenate x1 -> x0, other arithmetic: 0.99 us -> none  [on_device(): mixed_rows = jnp.concatenate([prompt_mix, stay_row, come_row], axis=0)]
    unnamed x7 -> x16, local copies, waits for them, and re-layouts: 2.87 us -> 2.6 us
  transfers between devices with their start and end apart: 4 -> 4, of which waited for: 2 -> 3; matrix products, arithmetic and copies ran while one was open for 3% -> 4% of each run, Pallas kernels for 14% -> 5%
where the time goes in v2:
time: 66.7 us; the launch traced here: 66.2 us
  waiting for transfers between devices  34.3 us (51%)
  starting transfers between devices  16.3 us (24%)
  Pallas kernels  11.6 us (17%)
  local copies, waits for them, and re-layouts  2.6 us (4%)
  between operations  1.39 us (2%)
    all_to_all x2, waiting for transfers between devices, exchange(): return lax.all_to_all(blocks, 'tp', 0, 0)  32.9 us
    all_to_all x2, starting transfers between devices, exchange(): return lax.all_to_all(blocks, 'tp', 0, 0)  10.4 us
    ppermute x2, starting transfers between devices, to_partner(): lax.ppermute(block, 'rep', [(i, (i + count // 2) % count) for i in range(...  5.9 us
    pallas_call x1, Pallas kernels, decode(): pl.pallas_call(decode_kernel, name='decode', compiler_params=pltpu.Compil...  3.29 us
    pallas_call x1, Pallas kernels, project(): pl.pallas_call(project_kernel, name='project', compiler_params=pltpu.Comp...  3.24 us
    pallas_call x1, Pallas kernels, prompt(): pl.pallas_call(functools.partial(prompt_kernel, block=block), name='promp...  3.01 us
    unnamed x16, local copies, waits for them, and re-layouts  2.6 us
    pallas_call x1, Pallas kernels, norm(): pl.pallas_call(norm_kernel, name='norm', compiler_params=pltpu.CompilerPa...  2.09 us
  transfers between devices with their start and end apart: 4, of which 3 were waited for; matrix products, arithmetic and copies ran while one was open for 4% of the time, Pallas kernels for 5%

profile of v2, /device:TPU:480, one launch (start us, length us, event | category | flops | bytes accessed | tf_op | source)
XLA Modules:
  0.0 66.2 jit_solution(14405492727570240791)
XLA Ops:
  0.6 0.0 copy-start.3
  0.6 0.0 copy-start.2
  0.7 0.0 copy-start.1
  0.7 3.3 %decode.1 = (bf16[1,2,260,256]{3,2,1,0:T(8,128)(2,1)}, bf16[1,256]{1,0:T(2,128)(2,1)S(1)}, bf16[1,256]{1,0:T(2,128)(2,1)S(1)}) custom-call(s32[64]{0:T(128)} %moving_hbm.1, s32[128]{0:T(128)} %cache_len_hbm.1, bf16[2,256]{1,0:T(2,128)(2,1)} %new_q_hbm.1, bf16[2,256]{1,0:T(2,128)(2,1)} %new_k_hbm.1, bf16[2,256]{1,0:T(2,128)(2,1)} %new_v_hbm.1, ...), custom_call_target="tpu_custom_call" | custom-call | tf_op jit(solution)/shard_map/decode/pallas_call | solution.py:151
  4.0 3.4 %collective-permute-start = (bf16[1,256]{1,0:T(2,128)(2,1)S(1)}, bf16[1,256]{1,0:T(2,128)(2,1)S(1)}, u32[]{:S(2)}, u32[]{:S(2)}) collective-permute-start(bf16[1,256]{1,0:T(2,128)(2,1)S(1)} %get-tuple-element.11), channel_id=1, source_target_pairs={{0,256},{8,264},{16,272},{24,280},{32,288},{40,296},{48,304},{56,3... | collective-permute-start | bytes 1544 | tf_op jit(solution)/shard_map/ppermute | solution.py:308
  8.0 1.4 %collective-permute-done.come_ref = bf16[1,256]{1,0:T(2,128)(2,1)S(1)} collective-permute-done((bf16[1,256]{1,0:T(2,128)(2,1)S(1)}, bf16[1,256]{1,0:T(2,128)(2,1)S(1)}, u32[]{:S(2)}, u32[]{:S(2)}) %collective-permute-start) | collective-permute-done | bytes 544 | tf_op jit(solution)/shard_map/ppermute | solution.py:308
  9.4 0.0 copy-done.3
  9.4 0.0 copy-done.2
  9.4 0.0 copy-done.1
  9.4 3.0 %prompt.1 = bf16[8,520,256]{2,1,0:T(8,128)(2,1)} custom-call(s32[1]{0:T(128)S(6)} %copy.21.length_ref, bf16[512,256]{1,0:T(8,128)(2,1)S(1)} %copy-done.1, bf16[512,256]{1,0:T(8,128)(2,1)S(1)} %copy-done.2, bf16[512,256]{1,0:T(8,128)(2,1)S(1)} %copy-done.3, bf16[1,256]{1,0:T(2,128)(2,1)S(1)} %get-tuple-element.10.stay_ref, ...), custom_call_target="tpu_custom_call" | custom-call | tf_op jit(solution)/shard_map/prompt/pallas_call | solution.py:208
  12.4 0.0 copy-start
  12.5 0.0 copy-start.4
  12.5 7.1 %all-to-all-start = ((bf16[8,520,256]{2,1,0:T(8,128)(2,1)}), bf16[8,520,256]{2,1,0:T(8,128)(2,1)S(1)}, u32[]{:S(2)}, u32[]{:S(2)}) async-start(bf16[8,520,256]{2,1,0:T(8,128)(2,1)} %prompt.1), calls=%async_computation | async-start | bytes 4259840 | tf_op jit(solution)/shard_map/all_to_all | solution.py:312
  19.5 2.5 %collective-permute-start.1 = (bf16[1,2,260,256]{3,2,1,0:T(8,128)(2,1)}, bf16[1,2,260,256]{3,2,1,0:T(8,128)(2,1)}, u32[]{:S(2)}, u32[]{:S(2)}) collective-permute-start(bf16[1,2,260,256]{3,2,1,0:T(8,128)(2,1)} %get-tuple-element.16), channel_id=1, source_target_pairs={{0,256},{8,264},{16,272},{24,280},{32,288},{40,296},{48,304},{56,3... | collective-permute-start | bytes 798728 | tf_op jit(solution)/shard_map/ppermute | solution.py:308
  22.0 27.8 %all-to-all-done.x_ref = bf16[8,520,256]{2,1,0:T(8,128)(2,1)S(1)} async-done(((bf16[8,520,256]{2,1,0:T(8,128)(2,1)}), bf16[8,520,256]{2,1,0:T(8,128)(2,1)S(1)}, u32[]{:S(2)}, u32[]{:S(2)}) %all-to-all-start) | async-done | bytes 2129952 | tf_op jit(solution)/shard_map/all_to_all | solution.py:312
  49.8 0.0 copy-done
  49.8 0.0 copy-done.4
  49.8 0.0 copy-start.5
  49.8 0.0 copy-start.6
  49.8 3.2 %project.1 = (bf16[514,256]{1,0:T(8,128)(2,1)S(1)}, f32[514,256]{1,0:T(8,128)}, f32[8,2,514]{2,1,0:T(2,128)}) custom-call(bf16[8,520,256]{2,1,0:T(8,128)(2,1)S(1)} %all-to-all-done.x_ref, bf16[2048,256]{1,0:T(8,128)(2,1)S(1)} %copy-done, f32[1,256]{1,0:T(1,128)S(1)} %bitcast.3, bf16[514,256]{1,0:T(8,128)(2,1)} %residual_hbm.1), custom_call_target="tpu_custom_call" | custom-call | tf_op jit(solution)/shard_map/project/pallas_call | solution.py:254
  53.1 3.4 %all-to-all-start.1 = ((f32[8,2,514]{2,1,0:T(2,128)}), f32[8,2,514]{2,1,0:T(2,128)S(1)}, u32[]{:S(2)}, u32[]{:S(2)}) async-start(f32[8,2,514]{2,1,0:T(2,128)} %get-tuple-element.13), calls=%async_computation.1 | async-start | bytes 81920 | tf_op jit(solution)/shard_map/all_to_all | solution.py:312
  56.4 0.0 collective-permute-done.1
  56.4 1.9 %copy.19 = bf16[1,2,260,256]{3,1,2,0:T(2,128)(2,1)} copy(bf16[1,2,260,256]{3,2,1,0:T(8,128)(2,1)} %collective-permute-done.1) | data formatting | bytes 532480
  58.3 0.7 %copy.20 = bf16[514,256]{1,0:T(8,128)(2,1)} copy(bf16[514,256]{1,0:T(8,128)(2,1)S(1)} %get-tuple-element.20) | data formatting | bytes 526336
  59.0 5.1 %all-to-all-done.1.stats_ref = f32[8,2,514]{2,1,0:T(2,128)S(1)} async-done(((f32[8,2,514]{2,1,0:T(2,128)}), f32[8,2,514]{2,1,0:T(2,128)S(1)}, u32[]{:S(2)}, u32[]{:S(2)}) %all-to-all-start.1) | async-done | bytes 32928 | tf_op jit(solution)/shard_map/all_to_all | solution.py:312
  64.1 0.0 copy-done.5
  64.1 0.0 copy-done.6
  64.1 2.1 %norm.1 = bf16[514,256]{1,0:T(8,128)(2,1)} custom-call(f32[8,2,514]{2,1,0:T(2,128)S(1)} %all-to-all-done.1.stats_ref, f32[514,256]{1,0:T(8,128)} %get-tuple-element.14.stream_hbm, f32[1,256]{1,0:T(1,128)S(1)} %bitcast.4, f32[1,256]{1,0:T(1,128)S(1)} %bitcast.5), custom_call_target="tpu_custom_call" | custom-call | tf_op jit(solution)/shard_map/norm/pallas_call | solution.py:295
Async XLA Ops:
  0.6 8.8 %copy-start.3 = (bf16[512,256]{1,0:T(8,128)(2,1)S(1)}, bf16[512,256]{1,0:T(8,128)(2,1)}, u32[]{:S(2)}) copy-start(bf16[512,256]{1,0:T(8,128)(2,1)} %v_ref.1) | copy-start | bytes 786436
  0.6 8.8 %copy-start.2 = (bf16[512,256]{1,0:T(8,128)(2,1)S(1)}, bf16[512,256]{1,0:T(8,128)(2,1)}, u32[]{:S(2)}) copy-start(bf16[512,256]{1,0:T(8,128)(2,1)} %k_ref.1) | copy-start | bytes 786436
  0.7 8.8 %copy-start.1 = (bf16[512,256]{1,0:T(8,128)(2,1)S(1)}, bf16[512,256]{1,0:T(8,128)(2,1)}, u32[]{:S(2)}) copy-start(bf16[512,256]{1,0:T(8,128)(2,1)} %q_ref.1) | copy-start | bytes 786436
  4.0 5.5 %collective-permute-start = (bf16[1,256]{1,0:T(2,128)(2,1)S(1)}, bf16[1,256]{1,0:T(2,128)(2,1)S(1)}, u32[]{:S(2)}, u32[]{:S(2)}) collective-permute-start(bf16[1,256]{1,0:T(2,128)(2,1)S(1)} %get-tuple-element.11), channel_id=1, source_target_pairs={{0,256},{8,264},{16,272},{24,280},{32,288},{40,296},{48,304},{56,3... | collective-permute-start | bytes 1544 | tf_op jit(solution)/shard_map/ppermute | solution.py:308
  12.4 37.4 %copy-start = (bf16[2048,256]{1,0:T(8,128)(2,1)S(1)}, bf16[2048,256]{1,0:T(8,128)(2,1)}, u32[]{:S(2)}) copy-start(bf16[2048,256]{1,0:T(8,128)(2,1)} %w_ref.1) | copy-start | bytes 3145732
  12.5 37.4 %copy-start.4 = (f32[256]{0:T(256)S(1)}, f32[256]{0:T(256)}, u32[]{:S(2)}) copy-start(f32[256]{0:T(256)} %param.28) | copy-start | bytes 3076
  12.5 37.3 %all-to-all-start = ((bf16[8,520,256]{2,1,0:T(8,128)(2,1)}), bf16[8,520,256]{2,1,0:T(8,128)(2,1)S(1)}, u32[]{:S(2)}, u32[]{:S(2)}) async-start(bf16[8,520,256]{2,1,0:T(8,128)(2,1)} %prompt.1), calls=%async_computation | async-start | bytes 4259840 | tf_op jit(solution)/shard_map/all_to_all | solution.py:312
  19.5 36.9 %collective-permute-start.1 = (bf16[1,2,260,256]{3,2,1,0:T(8,128)(2,1)}, bf16[1,2,260,256]{3,2,1,0:T(8,128)(2,1)}, u32[]{:S(2)}, u32[]{:S(2)}) collective-permute-start(bf16[1,2,260,256]{3,2,1,0:T(8,128)(2,1)} %get-tuple-element.16), channel_id=1, source_target_pairs={{0,256},{8,264},{16,272},{24,280},{32,288},{40,296},{48,304},{56,3... | collective-permute-start | bytes 798728 | tf_op jit(solution)/shard_map/ppermute | solution.py:308
  49.8 14.3 %copy-start.5 = (f32[256]{0:T(256)S(1)}, f32[256]{0:T(256)}, u32[]{:S(2)}) copy-start(f32[256]{0:T(256)} %param.30) | copy-start | bytes 3076
  49.8 14.3 %copy-start.6 = (f32[256]{0:T(256)S(1)}, f32[256]{0:T(256)}, u32[]{:S(2)}) copy-start(f32[256]{0:T(256)} %param.31) | copy-start | bytes 3076
  53.1 11.1 %all-to-all-start.1 = ((f32[8,2,514]{2,1,0:T(2,128)}), f32[8,2,514]{2,1,0:T(2,128)S(1)}, u32[]{:S(2)}, u32[]{:S(2)}) async-start(f32[8,2,514]{2,1,0:T(2,128)} %get-tuple-element.13), calls=%async_computation.1 | async-start | bytes 81920 | tf_op jit(solution)/shard_map/all_to_all | solution.py:312

commit v3 on v2

--- a/solution.py
+++ b/solution.py
@@ -53,6 +53,14 @@
     return lax.dot_general(a, b, (contract, ((), ())), precision=precision, preferred_element_type=F32)
 
 
+def core_of():
+    return lax.rem(lax.axis_index("rep"), 2)
+
+
+def side_of():
+    return lax.rem(lax.div(lax.axis_index("tp"), 2), 2)
+
+
 def head_slope(local_heads, head):
     tp = lax.axis_index("tp")
     slope = jnp.float32(LOG2E * 2.0 ** (-8.0 * (head + 1) / HEADS))
@@ -63,9 +71,18 @@
 
 
 def decode_kernel(
-    moving_hbm, cache_len_hbm, new_q_hbm, new_k_hbm, new_v_hbm, cache_k, cache_v,
-    window_out, stay_out, leave_out, moving, cache_len, new_q, new_k, new_v, body, sink, sems, small_sems,
+    moving_hbm, cache_len_hbm, new_q_hbm, new_k_hbm, new_v_hbm, cache_k, cache_v, weight_hbm, residual_hbm, bias_hbm,
+    window_out, stay_out, leave_out, packed_ref,
+    moving, cache_len, new_q, new_k, new_v, body, sink, sems, small_sems, residual_ref, bias_ref, pack_sems,
 ):
+    part = weight_hbm.shape[0] // 2
+    weight_copy = pltpu.make_async_copy(
+        weight_hbm.at[pl.ds(pl.multiple_of(core_of() * part, part), part)],
+        packed_ref.at[pl.ds(0, part)],
+        pack_sems.at[0],
+    )
+    residual_copy = pltpu.make_async_copy(residual_hbm, residual_ref, pack_sems.at[1])
+    bias_copy = pltpu.make_async_copy(bias_hbm, bias_ref, pack_sems.at[2])
     small = [
         pltpu.make_async_copy(source, target, small_sems.at[i])
         for i, (source, target) in enumerate((
@@ -104,6 +121,9 @@
     for pair in copies:
         for copy in pair:
             copy.start()
+    residual_copy.start()
+    bias_copy.start()
+    weight_copy.start()
 
     for copy in small[2:]:
         copy.wait()
@@ -145,9 +165,21 @@
         mixed = jnp.sum(jnp.where(own, mixed, 0.0), axis=0, keepdims=True)
         (leave_out, stay_out)[n][...] = mixed.astype(BF16)
 
-
-def decode(moving, cache_len, new_q, new_k, new_v, cache_k, cache_v):
+    residual_copy.wait()
+    bias_copy.wait()
+    half = (residual_ref.shape[0] - 2) // 2
+    lower, upper = residual_ref[: half + 8].astype(F32), residual_ref[half:].astype(F32)
+    upper = jnp.concatenate([upper, jnp.zeros((6, width), F32)], axis=0)
+    packed_ref[part : part + half + 8] = jnp.where(side_of() == 0, upper, lower).astype(BF16)
+    bias = bias_ref[...]
+    high = bias.astype(BF16).astype(F32)
+    packed_ref[part + half + 8 :] = jnp.where(row == 0, high, jnp.where(row == 1, bias - high, 0.0)).astype(BF16)
+    weight_copy.wait()
+
+
+def decode(moving, cache_len, new_q, new_k, new_v, cache_k, cache_v, weight, residual, bias):
     width = cache_k.shape[2]
+    tail = (residual.shape[0] - 2) // 2 + 16
     return pl.pallas_call(
         decode_kernel,
         name="decode",
@@ -156,9 +188,10 @@
             jax.ShapeDtypeStruct((1, 2, SPAN, width), BF16),
             jax.ShapeDtypeStruct((1, width), BF16),
             jax.ShapeDtypeStruct((1, width), BF16),
+            kept((weight.shape[0] // 2 + tail, width), BF16),
         ),
-        in_specs=[HBM] * 7,
-        out_specs=(VMEM, VMEM, VMEM),
+        in_specs=[HBM] * 10,
+        out_specs=(VMEM,) * 4,
         scratch_shapes=[
             pltpu.SMEM(moving.shape, jnp.int32),
             pltpu.SMEM(cache_len.shape, jnp.int32),
@@ -167,8 +200,11 @@
             pltpu.VMEM((2, 2, ROW_TILE, width), BF16),
             pltpu.SemaphoreType.DMA((2, 2, 2)),
             pltpu.SemaphoreType.DMA((5,)),
+            pltpu.VMEM(residual.shape, BF16),
+            pltpu.VMEM((1, width), F32),
+            pltpu.SemaphoreType.DMA((3,)),
         ],
-    )(*map(far, (moving, cache_len, new_q, new_k, new_v, cache_k, cache_v)))
+    )(*map(far, (moving, cache_len, new_q, new_k, new_v, cache_k, cache_v, weight, residual, bias)))
 
 
 def prompt_kernel(
@@ -193,9 +229,17 @@
             terms = jnp.exp2(scores - jnp.max(scores, axis=1, keepdims=True))
             weights = (terms / jnp.sum(terms, axis=1, keepdims=True)).astype(BF16)
             out_ref[first:keys, cols] = dot(weights, v_ref[:keys, cols], ((1,), (0,))).astype(BF16)
-        done = slice(first, keys if keys < rows else rows + 8)
         for member in range(out_hbm.shape[0]):
-            copy = pltpu.make_async_copy(out_ref.at[done], out_hbm.at[member, done], sems.at[step, member])
+            lower = member // 2 % 2 == 0
+            if lower and step == 0:
+                here, there = slice(0, block), slice(0, block)
+            elif lower:
+                here, there = slice(block, block + 8), slice(block, block + 8)
+            elif step == 1:
+                here, there = slice(block, rows + 8), slice(0, block + 8)
+            else:
+                continue
+            copy = pltpu.make_async_copy(out_ref.at[here], out_hbm.at[member, there], sems.at[step, member])
             copy.start()
             copies.append(copy)
     for copy in copies:
@@ -204,12 +248,12 @@
 
 def prompt(length, q, k, v, stay_row, come_row, members):
     rows, width = q.shape
-    block = 256
+    block = rows // 2
     return pl.pallas_call(
         functools.partial(prompt_kernel, block=block),
         name="prompt",
         compiler_params=pltpu.CompilerParams(vmem_limit_bytes=ROOM),
-        out_shape=placed((members, rows + 8, width), BF16),
+        out_shape=placed((members, block + 8, width), BF16),
         in_specs=[SMEM, VMEM, VMEM, VMEM, VMEM, VMEM],
         out_specs=HBM,
         scratch_shapes=[
@@ -219,93 +263,152 @@
     )(length, near(q), near(k), near(v), stay_row, come_row)
 
 
-def project_kernel(x_ref, w_ref, bias_ref, residual_hbm, hidden_ref, stream_hbm, stats_ref, residual_ref, sum_ref, sem):
-    copy = pltpu.make_async_copy(residual_hbm, residual_ref, sem)
-    copy.start()
-    sources, _, width = x_ref.shape
-    rows = sum_ref.shape[0]
+def project_kernel(
+    x_ref, w_ref, packed_ref, swapped_ref, bias_ref, residual_hbm,
+    own_hbm, pair_hbm, stats_ref, residual_ref, own_ref, pair_ref, sems,
+):
+    residual_copy = pltpu.make_async_copy(residual_hbm, residual_ref, sems.at[0])
+    residual_copy.start()
+    sources, rows, width = x_ref.shape
+    part = sources // 2
+    core, side = core_of(), side_of()
+    near_half, far_half = core * part, (1 - core) * part
     blocks = [slice(start, min(start + BLOCK, rows)) for start in range(0, rows, BLOCK)]
     for at in blocks:
-        sum_ref[at] = sum(
+        pair_ref[at] = sum(
+            dot(x_ref[near_half + s, at], packed_ref[s * width : (s + 1) * width], ((1,), (0,)))
+            + dot(x_ref[far_half + s, at], swapped_ref[s * width : (s + 1) * width], ((1,), (0,)))
+            for s in range(part)
+        )
+        own_ref[at] = sum(
             dot(x_ref[s, at], w_ref[s * width : (s + 1) * width], ((1,), (0,))) for s in range(sources)
         )
-    copy.wait()
-    for at in blocks:
+    residual_copy.wait()
+    extra = part * width
+    pair_bias = packed_ref[extra + rows :].astype(F32)
+    pair_bias = pair_bias[0:1] + pair_bias[1:2]
+    copies = []
+    for step, at in enumerate(blocks):
         size = at.stop - at.start
-        stream = sum_ref[at] + bias_ref[...] + residual_ref[at].astype(F32)
-        sum_ref[at] = stream
-        hidden_ref[at] = stream.astype(BF16)
-        mean = jnp.sum(stream, axis=1, keepdims=True) * (1.0 / width)
-        centered = stream - mean
-        spread = jnp.sum(centered * centered, axis=1, keepdims=True)
+        upper = residual_ref[at.start + rows - 8 : min(at.stop + rows - 8, residual_ref.shape[0])].astype(F32)
+        if upper.shape[0] < size:
+            upper = jnp.concatenate([upper, jnp.zeros((size - upper.shape[0], width), F32)], axis=0)
+        own = own_ref[at] + bias_ref[...] + jnp.where(side == 0, residual_ref[at].astype(F32), upper)
+        pair = pair_ref[at] + pair_bias + packed_ref[extra + at.start : extra + at.stop].astype(F32)
+        own_ref[at] = own
+        pair_ref[at] = pair
+        for k, (source, target) in enumerate(((own_ref, own_hbm), (pair_ref, pair_hbm))):
+            copy = pltpu.make_async_copy(source.at[at], target.at[at], sems.at[1 + 2 * step + k])
+            copy.start()
+            copies.append(copy)
+        mean = jnp.sum(own + pair, axis=1, keepdims=True) * (0.5 / width)
+        own_centered, pair_centered = own - mean, pair - mean
+        spread = jnp.sum(
+            own_centered * own_centered + pair_centered * pair_centered, axis=1, keepdims=True
+        )
         lane = lax.broadcasted_iota(jnp.int32, (size, HD), 1)
         table = jnp.where(lane == 0, mean, jnp.where(lane == 1, spread, 0.0))
         stats = table.T[:2]
-        for copy in range(stats_ref.shape[0]):
-            stats_ref[copy, :, at] = stats
-    out = pltpu.make_async_copy(sum_ref, stream_hbm, sem)
-    out.start()
-    out.wait()
-
-
-def project(gathered, weight, bias, residual):
-    sources = gathered.shape[0]
-    rows, width = residual.shape
+        for member in range(stats_ref.shape[0]):
+            stats_ref[member, :, at] = stats
+    for copy in copies:
+        copy.wait()
+
+
+def project(gathered, weight, packed, swapped, bias, residual):
+    sources, rows, width = gathered.shape
+    steps = -(-rows // BLOCK)
     return pl.pallas_call(
         project_kernel,
         name="project",
         compiler_params=pltpu.CompilerParams(vmem_limit_bytes=ROOM),
         out_shape=(
-            kept((rows, width), BF16),
+            placed((rows, width), F32),
             placed((rows, width), F32),
             placed((sources, 2, rows), F32),
         ),
-        in_specs=[VMEM, VMEM, VMEM, HBM],
-        out_specs=(VMEM, HBM, VMEM),
+        in_specs=[VMEM] * 5 + [HBM],
+        out_specs=(HBM, HBM, VMEM),
         scratch_shapes=[
-            pltpu.VMEM((rows, width), BF16),
+            pltpu.VMEM(residual.shape, BF16),
             pltpu.VMEM((rows, width), F32),
-            pltpu.SemaphoreType.DMA,
+            pltpu.VMEM((rows, width), F32),
+            pltpu.SemaphoreType.DMA((1 + 2 * steps,)),
         ],
-    )(near(gathered), near(weight), bias, far(residual))
-
-
-def norm_kernel(stats_ref, stream_hbm, gain_ref, shift_ref, out_ref, stream_ref, sem):
-    copy = pltpu.make_async_copy(stream_hbm, stream_ref, sem)
-    copy.start()
-    parts = stats_ref.shape[0]
-    rows, width = stream_ref.shape
-    means = stats_ref[:, 0, :]
-    mean = jnp.sum(means, axis=0, keepdims=True) * (1.0 / parts)
-    apart = means - mean
-    spread = jnp.sum(stats_ref[:, 1, :] + width * (apart * apart), axis=0, keepdims=True)
-    scale = lax.rsqrt(spread * (1.0 / (parts * width)) + EPSILON)
-    row = lax.broadcasted_iota(jnp.int32, (8, rows), 0)
-    table = jnp.where(row == 0, mean, jnp.where(row == 1, scale, 0.0))
-    copy.wait()
-    for start in range(0, rows, BLOCK):
-        at = slice(start, min(start + BLOCK, rows))
-        columns = table[:, at].T
-        out_ref[at] = (
-            (stream_ref[at] - columns[:, 0:1]) * columns[:, 1:2] * gain_ref[...] + shift_ref[...]
-        ).astype(BF16)
-
-
-def norm(stats, stream, gain, shift):
+    )(near(gathered), near(weight), near(packed), near(swapped), bias, far(residual))
+
+
+def norm_kernel(
+    stats_ref, own_hbm, come_hbm, gain_ref, shift_ref, hidden_ref, normed_ref, own_ref, come_ref, sems,
+):
+    copies = [
+        pltpu.make_async_copy(source, target, sems.at[i])
+        for i, (source, target) in enumerate(((own_hbm, own_ref), (come_hbm, come_ref)))
+    ]
+    for copy in copies:
+        copy.start()
+    members = stats_ref.shape[0]
+    rows, width = own_ref.shape
+    parts = members // 2
+    side = side_of()
+    tables = []
+    for half in range(2):
+        sources = [s for s in range(members) if s // 2 % 2 == half]
+        means = [stats_ref[s, 0:1, :] for s in sources]
+        mean = sum(means) * (1.0 / parts)
+        spread = sum(
+            stats_ref[s, 1:2, :] + (2 * width) * ((part - mean) * (part - mean))
+            for s, part in zip(sources, means)
+        )
+        scale = lax.rsqrt(spread * (1.0 / (members * width)) + EPSILON)
+        row = lax.broadcasted_iota(jnp.int32, (8, rows), 0)
+        tables.append(jnp.where(row == 0, mean, jnp.where(row == 1, scale, 0.0)))
+    for copy in copies:
+        copy.wait()
+    total = hidden_ref.shape[0]
+    for half, table in enumerate(tables):
+        first = half * (rows - 8)
+        used = rows - 8 if half == 0 else total - first
+        for start in range(0, used, BLOCK):
+            at = slice(start, min(start + BLOCK, used))
+            columns = table[:, at].T
+            own, come = own_ref[at], come_ref[at]
+            stream = jnp.where(side == half, own, come)
+            to = slice(first + at.start, first + at.stop)
+            hidden_ref[to] = stream.astype(BF16)
+            normed_ref[to] = (
+                (stream - columns[:, 0:1]) * columns[:, 1:2] * gain_ref[...] + shift_ref[...]
+            ).astype(BF16)
+
+
+def norm(stats, own, come, gain, shift, rows):
+    out = jax.ShapeDtypeStruct((rows, own.shape[1]), BF16)
     return pl.pallas_call(
         norm_kernel,
         name="norm",
         compiler_params=pltpu.CompilerParams(vmem_limit_bytes=ROOM),
-        out_shape=jax.ShapeDtypeStruct(stream.shape, BF16),
-        in_specs=[VMEM, HBM, VMEM, VMEM],
-        out_specs=VMEM,
-        scratch_shapes=[pltpu.VMEM(stream.shape, F32), pltpu.SemaphoreType.DMA],
-    )(near(stats), far(stream), gain, shift)
+        out_shape=(out, out),
+        in_specs=[VMEM, HBM, HBM, VMEM, VMEM],
+        out_specs=(VMEM, VMEM),
+        scratch_shapes=[
+            pltpu.VMEM(own.shape, F32),
+            pltpu.VMEM(own.shape, F32),
+            pltpu.SemaphoreType.DMA((2,)),
+        ],
+    )(near(stats), far(own), far(come), gain, shift)
 
 
 def to_partner(block):
     count = lax.axis_size("rep")
     return lax.ppermute(block, "rep", [(i, (i + count // 2) % count) for i in range(count)])
+
+
+def to_pair(block):
+    return lax.ppermute(block, "tp", [(i, i ^ 2) for i in range(lax.axis_size("tp"))])
+
+
+def to_sibling(block):
+    return lax.ppermute(block, "rep", [(i, i ^ 1) for i in range(lax.axis_size("rep"))])
 
 
 def exchange(blocks):
@@ -320,17 +423,23 @@
     prompt_q, prompt_k, prompt_v, prompt_len, cache_keys, cache_values, new_q, new_k, new_v,
     cache_len, moving, out_weight, out_bias, residual, ln_gain, ln_shift,
 ):
-    window, stay_row, leave_row = decode(
-        moving, cache_len, new_q, new_k, new_v, cache_keys, cache_values
+    window, stay_row, leave_row, packed = decode(
+        moving, cache_len, new_q, new_k, new_v, cache_keys, cache_values, out_weight, residual, out_bias[None]
     )
     come_row = to_partner(leave_row)
-    window, leave_row = lax.optimization_barrier((window, leave_row))
+    packed = to_pair(packed)
+    swapped = to_sibling(packed)
     moved_window = to_partner(window)
     mixed = prompt(
         prompt_len, prompt_q, prompt_k, prompt_v, stay_row, come_row, lax.axis_size("tp")
     )
-    hidden_out, stream, stats = project(exchange(mixed), out_weight, out_bias[None], residual)
-    normed = norm(exchange(stats), stream, ln_gain[None], ln_shift[None])
+    own, pair, stats = project(
+        exchange(mixed), out_weight, packed, swapped, out_bias[None], residual
+    )
+    stats = exchange(stats)
+    hidden_out, normed = norm(
+        stats, own, to_pair(pair), ln_gain[None], ln_shift[None], residual.shape[0]
+    )
     return (hidden_out, normed, moved_window)
 
 

time: 66.7 us -> 63.1 us (0.946)
  waiting for transfers between devices: 34.3 us -> 22.7 us
  starting transfers between devices: 16.3 us -> 24.8 us
  local copies, waits for them, and re-layouts: 2.6 us -> 1.65 us
    all_to_all x2, waiting for transfers between devices: 32.9 us -> 19.9 us  [exchange(): return lax.all_to_all(blocks, 'tp', 0, 0)]
    ppermute x0 -> x3, starting transfers between devices: none -> 7.33 us  [the longest x2 5.4 us: to_pair(): lax.ppermute(block, 'tp', [(i, i ^ 2) for i in range(lax.axis_size('tp'))])]
    ppermute x2, waiting for transfers between devices: 1.41 us -> 2.79 us  [to_partner(): lax.ppermute(block, 'rep', [(i, (i + count // 2) % count) for i in range(...]
    all_to_all x2, starting transfers between devices: 10.4 us -> 11.5 us  [exchange(): return lax.all_to_all(blocks, 'tp', 0, 0)]
    unnamed x16 -> x17, local copies, waits for them, and re-layouts: 2.6 us -> 1.65 us
  transfers between devices with their start and end apart: 4 -> 7, of which waited for: 3 -> 4; matrix products, arithmetic and copies ran while one was open for 4% -> 1% of each run, Pallas kernels for 5% -> 4%
where the time goes in v3:
time: 63.1 us; the launch traced here: 62.6 us
  starting transfers between devices  24.8 us (39%)
  waiting for transfers between devices  22.7 us (36%)
  Pallas kernels  12 us (19%)
  local copies, waits for them, and re-layouts  1.65 us (3%)
  between operations  1.42 us (2%)
    all_to_all x2, waiting for transfers between devices, exchange(): return lax.all_to_all(blocks, 'tp', 0, 0)  19.9 us
    all_to_all x2, starting transfers between devices, exchange(): return lax.all_to_all(blocks, 'tp', 0, 0)  11.5 us
    ppermute x2, starting transfers between devices, to_partner(): lax.ppermute(block, 'rep', [(i, (i + count // 2) % count) for i in range(...  5.95 us
    ppermute x2, starting transfers between devices, to_pair(): lax.ppermute(block, 'tp', [(i, i ^ 2) for i in range(lax.axis_size('tp'))])  5.4 us
    pallas_call x1, Pallas kernels, decode(): pl.pallas_call(decode_kernel, name='decode', compiler_params=pltpu.Compil...  3.82 us
    pallas_call x1, Pallas kernels, project(): pl.pallas_call(project_kernel, name='project', compiler_params=pltpu.Comp...  3.32 us
    ppermute x2, waiting for transfers between devices, to_partner(): lax.ppermute(block, 'rep', [(i, (i + count // 2) % count) for i in range(...  2.79 us
    pallas_call x1, Pallas kernels, prompt(): pl.pallas_call(functools.partial(prompt_kernel, block=block), name='promp...  2.76 us
  transfers between devices with their start and end apart: 7, of which 4 were waited for; matrix products, arithmetic and copies ran while one was open for 1% of the time, Pallas kernels for 4%

profile of v3, /device:TPU:480, one launch (start us, length us, event | category | flops | bytes accessed | tf_op | source)
XLA Modules:
  0.0 62.6 jit_solution(15588934655952160873)
XLA Ops:
  0.6 0.0 copy-start.1
  0.6 0.0 copy-start.2
  0.7 0.0 copy-start.3
  0.7 3.8 %decode.1 = (bf16[1,2,260,256]{3,2,1,0:T(8,128)(2,1)}, bf16[1,256]{1,0:T(2,128)(2,1)S(1)}, bf16[1,256]{1,0:T(2,128)(2,1)S(1)}, bf16[1296,256]{1,0:T(8,128)(2,1)S(1)}) custom-call(s32[64]{0:T(128)} %moving_hbm.1, s32[128]{0:T(128)} %cache_len_hbm.1, bf16[2,256]{1,0:T(2,128)(2,1)} %new_q_hbm.1, bf16[2,256]{1,0:T(2,128)(2,1)} %new_k_hbm.1, ...), custom_call_target="tpu_custom_call" | custom-call | tf_op jit(solution)/shard_map/decode/pallas_call | solution.py:183
  4.5 3.5 %collective-permute-start.1 = (bf16[1296,256]{1,0:T(8,128)(2,1)S(1)}, bf16[1296,256]{1,0:T(8,128)(2,1)S(1)}, u32[]{:S(2)}, u32[]{:S(2)}) collective-permute-start(bf16[1296,256]{1,0:T(8,128)(2,1)S(1)} %get-tuple-element.14), channel_id=1, source_target_pairs={{0,2},{1,3},{2,0},{3,1},{4,6},{5,7},{6,4},{7,5},{8,10},{9,11},{10,... | collective-permute-start | bytes 1990664 | tf_op jit(solution)/shard_map/ppermute | solution.py:407
  8.0 3.4 %collective-permute-start = (bf16[1,256]{1,0:T(2,128)(2,1)S(1)}, bf16[1,256]{1,0:T(2,128)(2,1)S(1)}, u32[]{:S(2)}, u32[]{:S(2)}) collective-permute-start(bf16[1,256]{1,0:T(2,128)(2,1)S(1)} %get-tuple-element.13), channel_id=1, source_target_pairs={{0,256},{8,264},{16,272},{24,280},{32,288},{40,296},{48,304},{56,3... | collective-permute-start | bytes 1544 | tf_op jit(solution)/shard_map/ppermute | solution.py:403
  12.0 1.4 %collective-permute-done.come_ref = bf16[1,256]{1,0:T(2,128)(2,1)S(1)} collective-permute-done((bf16[1,256]{1,0:T(2,128)(2,1)S(1)}, bf16[1,256]{1,0:T(2,128)(2,1)S(1)}, u32[]{:S(2)}, u32[]{:S(2)}) %collective-permute-start) | collective-permute-done | bytes 544 | tf_op jit(solution)/shard_map/ppermute | solution.py:403
  13.4 0.0 copy-done.1
  13.5 0.0 copy-done.2
  13.5 0.0 copy-done.3
  13.5 2.8 %prompt.1 = bf16[8,264,256]{2,1,0:T(8,128)(2,1)} custom-call(s32[1]{0:T(128)S(6)} %copy.20.length_ref, bf16[512,256]{1,0:T(8,128)(2,1)S(1)} %copy-done.1, bf16[512,256]{1,0:T(8,128)(2,1)S(1)} %copy-done.2, bf16[512,256]{1,0:T(8,128)(2,1)S(1)} %copy-done.3, bf16[1,256]{1,0:T(2,128)(2,1)S(1)} %get-tuple-element.12.stay_ref, ...), custom_call_target="tpu_custom_call" | custom-call | tf_op jit(solution)/shard_map/prompt/pallas_call | solution.py:252
  16.2 0.0 copy-start
  16.2 0.0 copy-start.4
  16.3 6.8 %all-to-all-start = ((bf16[8,264,256]{2,1,0:T(8,128)(2,1)}), bf16[8,264,256]{2,1,0:T(8,128)(2,1)S(1)}, u32[]{:S(2)}, u32[]{:S(2)}) async-start(bf16[8,264,256]{2,1,0:T(8,128)(2,1)} %prompt.1), calls=%async_computation | async-start | bytes 2162688 | tf_op jit(solution)/shard_map/all_to_all | solution.py:415
  23.0 0.0 copy-start.5
  23.0 0.0 copy-start.6
  23.1 0.0 collective-permute-done.1.packed_ref
  23.1 1.9 %collective-permute-start.2 = (bf16[1296,256]{1,0:T(8,128)(2,1)S(1)}, bf16[1296,256]{1,0:T(8,128)(2,1)S(1)}, u32[]{:S(2)}, u32[]{:S(2)}) collective-permute-start(bf16[1296,256]{1,0:T(8,128)(2,1)S(1)} %collective-permute-done.1.packed_ref), channel_id=1, source_target_pairs={{0,8},{8,0},{16,24},{24,16},{32,40},{40,32},{48,56},{56,48},{64,72... | collective-permute-start | bytes 1990664 | tf_op jit(solution)/shard_map/ppermute | solution.py:411
  25.0 14.5 %all-to-all-done.x_ref = bf16[8,264,256]{2,1,0:T(8,128)(2,1)S(1)} async-done(((bf16[8,264,256]{2,1,0:T(8,128)(2,1)}), bf16[8,264,256]{2,1,0:T(8,128)(2,1)S(1)}, u32[]{:S(2)}, u32[]{:S(2)}) %all-to-all-start) | async-done | bytes 1081376 | tf_op jit(solution)/shard_map/all_to_all | solution.py:415
  39.5 0.0 collective-permute-done.2.swapped_ref
  39.5 0.0 copy-done
  39.5 0.0 copy-done.4
  39.5 3.3 %project.1 = (f32[264,256]{1,0:T(8,128)}, f32[264,256]{1,0:T(8,128)}, f32[8,2,264]{2,1,0:T(2,128)}) custom-call(bf16[8,264,256]{2,1,0:T(8,128)(2,1)S(1)} %all-to-all-done.x_ref, bf16[2048,256]{1,0:T(8,128)(2,1)S(1)} %copy-done, bf16[1296,256]{1,0:T(8,128)(2,1)S(1)} %collective-permute-done.1.packed_ref, ...), custom_call_target="tpu_custom_call" | custom-call | tf_op jit(solution)/shard_map/project/pallas_call | solution.py:321
  42.8 1.9 %collective-permute-start.3 = (f32[264,256]{1,0:T(8,128)}, f32[264,256]{1,0:T(8,128)S(1)}, u32[]{:S(2)}, u32[]{:S(2)}) collective-permute-start(f32[264,256]{1,0:T(8,128)} %get-tuple-element.17), channel_id=1, source_target_pairs={{0,2},{1,3},{2,0},{3,1},{4,6},{5,7},{6,4},{7,5},{8,10},{9,11},{10,... | collective-permute-start | bytes 811016 | tf_op jit(solution)/shard_map/ppermute | solution.py:407
  44.7 2.5 %collective-permute-start.4 = (bf16[1,2,260,256]{3,2,1,0:T(8,128)(2,1)}, bf16[1,2,260,256]{3,2,1,0:T(8,128)(2,1)S(1)}, u32[]{:S(2)}, u32[]{:S(2)}) collective-permute-start(bf16[1,2,260,256]{3,2,1,0:T(8,128)(2,1)} %get-tuple-element.20), channel_id=1, source_target_pairs={{0,256},{8,264},{16,272},{24,280},{32,288},{40,296},{48,304},{56,3... | collective-permute-start | bytes 798728 | tf_op jit(solution)/shard_map/ppermute | solution.py:403
  47.3 4.8 %all-to-all-start.1 = ((f32[8,2,264]{2,1,0:T(2,128)}), f32[8,2,264]{2,1,0:T(2,128)S(1)}, u32[]{:S(2)}, u32[]{:S(2)}) async-start(f32[8,2,264]{2,1,0:T(2,128)} %get-tuple-element.15), calls=%async_computation.1 | async-start | bytes 49152 | tf_op jit(solution)/shard_map/all_to_all | solution.py:415
  52.0 1.4 %collective-permute-done.4 = bf16[1,2,260,256]{3,2,1,0:T(8,128)(2,1)S(1)} collective-permute-done((bf16[1,2,260,256]{3,2,1,0:T(8,128)(2,1)}, bf16[1,2,260,256]{3,2,1,0:T(8,128)(2,1)S(1)}, u32[]{:S(2)}, u32[]{:S(2)}) %collective-permute-start.4) | collective-permute-done | bytes 266272 | tf_op jit(solution)/shard_map/ppermute | solution.py:403
  53.4 0.9 %copy.19 = bf16[1,2,260,256]{3,1,2,0:T(2,128)(2,1)} copy(bf16[1,2,260,256]{3,2,1,0:T(8,128)(2,1)S(1)} %collective-permute-done.4) | data formatting | bytes 532480
  54.3 5.4 %all-to-all-done.1.stats_ref = f32[8,2,264]{2,1,0:T(2,128)S(1)} async-done(((f32[8,2,264]{2,1,0:T(2,128)}), f32[8,2,264]{2,1,0:T(2,128)S(1)}, u32[]{:S(2)}, u32[]{:S(2)}) %all-to-all-start.1) | async-done | bytes 16928 | tf_op jit(solution)/shard_map/all_to_all | solution.py:415
  59.8 0.0 collective-permute-done.3.come_hbm
  59.8 0.0 copy-start.7
  59.8 0.7 %copy-done.7 = f32[264,256]{1,0:T(8,128)} copy-done((f32[264,256]{1,0:T(8,128)}, f32[264,256]{1,0:T(8,128)S(1)}, u32[]{:S(2)}) %copy-start.7) | copy-done | bytes 270360
  60.5 0.0 copy-done.5
  60.5 0.0 copy-done.6
  60.5 2.1 %norm.1 = (bf16[514,256]{1,0:T(8,128)(2,1)}, bf16[514,256]{1,0:T(8,128)(2,1)}) custom-call(f32[8,2,264]{2,1,0:T(2,128)S(1)} %all-to-all-done.1.stats_ref, f32[264,256]{1,0:T(8,128)} %get-tuple-element.16.own_hbm, f32[264,256]{1,0:T(8,128)} %copy-done.7, f32[1,256]{1,0:T(1,128)S(1)} %bitcast.5, f32[1,256]{1,0:T(1,128)S(1)} %bitcast.6), custom_call_target="tpu_custom_call" | custom-call | tf_op jit(solution)/shard_map/norm/pallas_call | solution.py:386
Async XLA Ops:
  0.6 12.8 %copy-start.1 = (bf16[512,256]{1,0:T(8,128)(2,1)S(1)}, bf16[512,256]{1,0:T(8,128)(2,1)}, u32[]{:S(2)}) copy-start(bf16[512,256]{1,0:T(8,128)(2,1)} %q_ref.1) | copy-start | bytes 786436
  0.6 12.8 %copy-start.2 = (bf16[512,256]{1,0:T(8,128)(2,1)S(1)}, bf16[512,256]{1,0:T(8,128)(2,1)}, u32[]{:S(2)}) copy-start(bf16[512,256]{1,0:T(8,128)(2,1)} %k_ref.1) | copy-start | bytes 786436
  0.7 12.8 %copy-start.3 = (bf16[512,256]{1,0:T(8,128)(2,1)S(1)}, bf16[512,256]{1,0:T(8,128)(2,1)}, u32[]{:S(2)}) copy-start(bf16[512,256]{1,0:T(8,128)(2,1)} %v_ref.1) | copy-start | bytes 786436
  4.5 18.6 %collective-permute-start.1 = (bf16[1296,256]{1,0:T(8,128)(2,1)S(1)}, bf16[1296,256]{1,0:T(8,128)(2,1)S(1)}, u32[]{:S(2)}, u32[]{:S(2)}) collective-permute-start(bf16[1296,256]{1,0:T(8,128)(2,1)S(1)} %get-tuple-element.14), channel_id=1, source_target_pairs={{0,2},{1,3},{2,0},{3,1},{4,6},{5,7},{6,4},{7,5},{8,10},{9,11},{10,... | collective-permute-start | bytes 1990664 | tf_op jit(solution)/shard_map/ppermute | solution.py:407
  8.0 5.5 %collective-permute-start = (bf16[1,256]{1,0:T(2,128)(2,1)S(1)}, bf16[1,256]{1,0:T(2,128)(2,1)S(1)}, u32[]{:S(2)}, u32[]{:S(2)}) collective-permute-start(bf16[1,256]{1,0:T(2,128)(2,1)S(1)} %get-tuple-element.13), channel_id=1, source_target_pairs={{0,256},{8,264},{16,272},{24,280},{32,288},{40,296},{48,304},{56,3... | collective-permute-start | bytes 1544 | tf_op jit(solution)/shard_map/ppermute | solution.py:403
  16.2 23.2 %copy-start = (bf16[2048,256]{1,0:T(8,128)(2,1)S(1)}, bf16[2048,256]{1,0:T(8,128)(2,1)}, u32[]{:S(2)}) copy-start(bf16[2048,256]{1,0:T(8,128)(2,1)} %w_ref.1) | copy-start | bytes 3145732
  16.2 23.2 %copy-start.4 = (f32[256]{0:T(256)S(1)}, f32[256]{0:T(256)}, u32[]{:S(2)}) copy-start(f32[256]{0:T(256)} %param.28) | copy-start | bytes 3076
  16.3 23.2 %all-to-all-start = ((bf16[8,264,256]{2,1,0:T(8,128)(2,1)}), bf16[8,264,256]{2,1,0:T(8,128)(2,1)S(1)}, u32[]{:S(2)}, u32[]{:S(2)}) async-start(bf16[8,264,256]{2,1,0:T(8,128)(2,1)} %prompt.1), calls=%async_computation | async-start | bytes 2162688 | tf_op jit(solution)/shard_map/all_to_all | solution.py:415
  23.0 37.5 %copy-start.5 = (f32[256]{0:T(256)S(1)}, f32[256]{0:T(256)}, u32[]{:S(2)}) copy-start(f32[256]{0:T(256)} %param.30) | copy-start | bytes 3076
  23.0 37.5 %copy-start.6 = (f32[256]{0:T(256)S(1)}, f32[256]{0:T(256)}, u32[]{:S(2)}) copy-start(f32[256]{0:T(256)} %param.31) | copy-start | bytes 3076
  23.1 16.4 %collective-permute-start.2 = (bf16[1296,256]{1,0:T(8,128)(2,1)S(1)}, bf16[1296,256]{1,0:T(8,128)(2,1)S(1)}, u32[]{:S(2)}, u32[]{:S(2)}) collective-permute-start(bf16[1296,256]{1,0:T(8,128)(2,1)S(1)} %collective-permute-done.1.packed_ref), channel_id=1, source_target_pairs={{0,8},{8,0},{16,24},{24,16},{32,40},{40,32},{48,56},{56,48},{64,72... | collective-permute-start | bytes 1990664 | tf_op jit(solution)/shard_map/ppermute | solution.py:411
  42.8 17.0 %collective-permute-start.3 = (f32[264,256]{1,0:T(8,128)}, f32[264,256]{1,0:T(8,128)S(1)}, u32[]{:S(2)}, u32[]{:S(2)}) collective-permute-start(f32[264,256]{1,0:T(8,128)} %get-tuple-element.17), channel_id=1, source_target_pairs={{0,2},{1,3},{2,0},{3,1},{4,6},{5,7},{6,4},{7,5},{8,10},{9,11},{10,... | collective-permute-start | bytes 811016 | tf_op jit(solution)/shard_map/ppermute | solution.py:407
  44.7 8.7 %collective-permute-start.4 = (bf16[1,2,260,256]{3,2,1,0:T(8,128)(2,1)}, bf16[1,2,260,256]{3,2,1,0:T(8,128)(2,1)S(1)}, u32[]{:S(2)}, u32[]{:S(2)}) collective-permute-start(bf16[1,2,260,256]{3,2,1,0:T(8,128)(2,1)} %get-tuple-element.20), channel_id=1, source_target_pairs={{0,256},{8,264},{16,272},{24,280},{32,288},{40,296},{48,304},{56,3... | collective-permute-start | bytes 798728 | tf_op jit(solution)/shard_map/ppermute | solution.py:403
  47.3 12.5 %all-to-all-start.1 = ((f32[8,2,264]{2,1,0:T(2,128)}), f32[8,2,264]{2,1,0:T(2,128)S(1)}, u32[]{:S(2)}, u32[]{:S(2)}) async-start(f32[8,2,264]{2,1,0:T(2,128)} %get-tuple-element.15), calls=%async_computation.1 | async-start | bytes 49152 | tf_op jit(solution)/shard_map/all_to_all | solution.py:415
  59.8 0.7 %copy-start.7 = (f32[264,256]{1,0:T(8,128)}, f32[264,256]{1,0:T(8,128)S(1)}, u32[]{:S(2)}) copy-start(f32[264,256]{1,0:T(8,128)S(1)} %collective-permute-done.3.come_hbm) | copy-start | bytes 811012

commit v4 on v3

--- a/solution.py
+++ b/solution.py
@@ -72,7 +72,7 @@
 
 def decode_kernel(
     moving_hbm, cache_len_hbm, new_q_hbm, new_k_hbm, new_v_hbm, cache_k, cache_v, weight_hbm, residual_hbm, bias_hbm,
-    window_out, stay_out, leave_out, packed_ref,
+    window_out, stay_out, packed_ref,
     moving, cache_len, new_q, new_k, new_v, body, sink, sems, small_sems, residual_ref, bias_ref, pack_sems,
 ):
     part = weight_hbm.shape[0] // 2
@@ -151,19 +151,23 @@
             )
             top = jnp.where(row < SINK, sink[n, kv].astype(F32)[:8], rolled[:8])
             tail = jnp.where(row == SPAN - 1 - WIN, newest(new), rolled[WIN : WIN + 8])
-            window = jnp.concatenate([top, rolled[8:WIN], tail, rolled[WIN + 8 :]], axis=0).astype(BF16)
-            if n == 0:
-                window_out[0, kv] = window[:SPAN]
-            windows.append(window)
+            windows.append(jnp.concatenate([top, rolled[8:WIN], tail, rolled[WIN + 8 :]], axis=0))
+        keys, values = (window.astype(BF16) for window in windows)
         query = jnp.where(own, newest(new_q), 0.0).astype(BF16)
-        scores = dot(query, windows[0], ((1,), (1,))) * SCALE
+        scores = dot(query, keys, ((1,), (1,))) * SCALE
         distance = jnp.where(column < SINK, lengths[n] - column, SPAN - 1 - column).astype(F32)
         scores = jnp.where(column < SPAN, scores - slopes * distance, MASKED)
         terms = jnp.exp2(scores - jnp.max(scores, axis=1, keepdims=True))
         weights = (terms / jnp.sum(terms, axis=1, keepdims=True)).astype(BF16)
-        mixed = dot(weights, windows[1], ((1,), (0,)))
+        mixed = dot(weights, values, ((1,), (0,)))
         mixed = jnp.sum(jnp.where(own, mixed, 0.0), axis=0, keepdims=True)
-        (leave_out, stay_out)[n][...] = mixed.astype(BF16)
+        if n == 0:
+            window_out[0, 0, :WIN] = keys[:WIN]
+            last = jnp.where(row == SPAN - WIN, mixed, windows[0][WIN : WIN + 8])
+            window_out[0, 0, WIN:] = last.astype(BF16)
+            window_out[0, 1] = values[: WIN + 8]
+        else:
+            stay_out[...] = mixed.astype(BF16)
 
     residual_copy.wait()
     bias_copy.wait()
@@ -185,13 +189,12 @@
         name="decode",
         compiler_params=pltpu.CompilerParams(vmem_limit_bytes=ROOM),
         out_shape=(
-            jax.ShapeDtypeStruct((1, 2, SPAN, width), BF16),
-            jax.ShapeDtypeStruct((1, width), BF16),
+            placed((1, 2, WIN + 8, width), BF16),
             jax.ShapeDtypeStruct((1, width), BF16),
             kept((weight.shape[0] // 2 + tail, width), BF16),
         ),
         in_specs=[HBM] * 10,
-        out_specs=(VMEM,) * 4,
+        out_specs=(VMEM,) * 3,
         scratch_shapes=[
             pltpu.SMEM(moving.shape, jnp.int32),
             pltpu.SMEM(cache_len.shape, jnp.int32),
@@ -208,12 +211,9 @@
 
 
 def prompt_kernel(
-    length_ref, q_ref, k_ref, v_ref, stay_ref, come_ref, out_hbm, out_ref, sems, *, block,
+    length_ref, q_ref, k_ref, v_ref, out_hbm, out_ref, sems, *, block,
 ):
     rows, width = q_ref.shape
-    row = lax.broadcasted_iota(jnp.int32, (8, width), 0)
-    served = jnp.where(row == 0, stay_ref[...].astype(F32), jnp.where(row == 1, come_ref[...].astype(F32), 0.0))
-    out_ref[rows:] = served.astype(BF16)
     length = length_ref[0]
     copies = []
     for step, first in enumerate(range(0, rows, block)):
@@ -236,7 +236,7 @@
             elif lower:
                 here, there = slice(block, block + 8), slice(block, block + 8)
             elif step == 1:
-                here, there = slice(block, rows + 8), slice(0, block + 8)
+                here, there = slice(block, rows), slice(0, block)
             else:
                 continue
             copy = pltpu.make_async_copy(out_ref.at[here], out_hbm.at[member, there], sems.at[step, member])
@@ -246,7 +246,7 @@
         copy.wait()
 
 
-def prompt(length, q, k, v, stay_row, come_row, members):
+def prompt(length, q, k, v, members):
     rows, width = q.shape
     block = rows // 2
     return pl.pallas_call(
@@ -254,13 +254,44 @@
         name="prompt",
         compiler_params=pltpu.CompilerParams(vmem_limit_bytes=ROOM),
         out_shape=placed((members, block + 8, width), BF16),
-        in_specs=[SMEM, VMEM, VMEM, VMEM, VMEM, VMEM],
+        in_specs=[SMEM, VMEM, VMEM, VMEM],
         out_specs=HBM,
         scratch_shapes=[
-            pltpu.VMEM((rows + 8, width), BF16),
+            pltpu.VMEM((rows, width), BF16),
             pltpu.SemaphoreType.DMA((rows // block, members)),
         ],
-    )(length, near(q), near(k), near(v), stay_row, come_row)
+    )(length, near(q), near(k), near(v))
+
+
+def insert_kernel(stay_ref, come_ref, given, rows_hbm, tile, sems):
+    del given
+    row = lax.broadcasted_iota(jnp.int32, tile.shape, 0)
+    come = come_ref[0, 0, WIN:].astype(F32)[SPAN - WIN : SPAN - WIN + 1]
+    tile[...] = jnp.where(row == 0, stay_ref[...].astype(F32), jnp.where(row == 1, come, 0.0)).astype(BF16)
+    members, rows, _ = rows_hbm.shape
+    copies = [
+        pltpu.make_async_copy(tile, rows_hbm.at[member, pl.ds(rows - 8, 8)], sems.at[member])
+        for member in range(members)
+        if member // 2 % 2 == 1
+    ]
+    for copy in copies:
+        copy.start()
+    for copy in copies:
+        copy.wait()
+
+
+def insert(stay_row, come, rows):
+    members, _, width = rows.shape
+    return pl.pallas_call(
+        insert_kernel,
+        name="insert",
+        compiler_params=pltpu.CompilerParams(vmem_limit_bytes=ROOM),
+        out_shape=placed(rows.shape, rows.dtype),
+        in_specs=[VMEM, VMEM, HBM],
+        out_specs=HBM,
+        scratch_shapes=[pltpu.VMEM((8, width), BF16), pltpu.SemaphoreType.DMA((members,))],
+        input_output_aliases={2: 0},
+    )(stay_row, near(come), far(rows))
 
 
 def project_kernel(
@@ -339,14 +370,10 @@
 
 
 def norm_kernel(
-    stats_ref, own_hbm, come_hbm, gain_ref, shift_ref, hidden_ref, normed_ref, own_ref, come_ref, sems,
+    stats_ref, own_hbm, come_ref, gain_ref, shift_ref, hidden_ref, normed_ref, own_ref, sem,
 ):
-    copies = [
-        pltpu.make_async_copy(source, target, sems.at[i])
-        for i, (source, target) in enumerate(((own_hbm, own_ref), (come_hbm, come_ref)))
-    ]
-    for copy in copies:
-        copy.start()
+    copy = pltpu.make_async_copy(own_hbm, own_ref, sem)
+    copy.start()
     members = stats_ref.shape[0]
     rows, width = own_ref.shape
     parts = members // 2
@@ -363,8 +390,7 @@
         scale = lax.rsqrt(spread * (1.0 / (members * width)) + EPSILON)
         row = lax.broadcasted_iota(jnp.int32, (8, rows), 0)
         tables.append(jnp.where(row == 0, mean, jnp.where(row == 1, scale, 0.0)))
-    for copy in copies:
-        copy.wait()
+    copy.wait()
     total = hidden_ref.shape[0]
     for half, table in enumerate(tables):
         first = half * (rows - 8)
@@ -388,14 +414,10 @@
         name="norm",
         compiler_params=pltpu.CompilerParams(vmem_limit_bytes=ROOM),
         out_shape=(out, out),
-        in_specs=[VMEM, HBM, HBM, VMEM, VMEM],
+        in_specs=[VMEM, HBM, VMEM, VMEM, VMEM],
         out_specs=(VMEM, VMEM),
-        scratch_shapes=[
-            pltpu.VMEM(own.shape, F32),
-            pltpu.VMEM(own.shape, F32),
-            pltpu.SemaphoreType.DMA((2,)),
-        ],
-    )(near(stats), far(own), far(come), gain, shift)
+        scratch_shapes=[pltpu.VMEM(own.shape, F32), pltpu.SemaphoreType.DMA],
+    )(near(stats), far(own), near(come), gain, shift)
 
 
 def to_partner(block):
@@ -423,16 +445,15 @@
     prompt_q, prompt_k, prompt_v, prompt_len, cache_keys, cache_values, new_q, new_k, new_v,
     cache_len, moving, out_weight, out_bias, residual, ln_gain, ln_shift,
 ):
-    window, stay_row, leave_row, packed = decode(
+    window, stay_row, packed = decode(
         moving, cache_len, new_q, new_k, new_v, cache_keys, cache_values, out_weight, residual, out_bias[None]
     )
-    come_row = to_partner(leave_row)
+    come = to_partner(window)
     packed = to_pair(packed)
     swapped = to_sibling(packed)
-    moved_window = to_partner(window)
-    mixed = prompt(
-        prompt_len, prompt_q, prompt_k, prompt_v, stay_row, come_row, lax.axis_size("tp")
-    )
+    mixed = prompt(prompt_len, prompt_q, prompt_k, prompt_v, lax.axis_size("tp"))
+    mixed = insert(stay_row, come, mixed)
+    moved_window = come[:, :, :SPAN]
     own, pair, stats = project(
         exchange(mixed), out_weight, packed, swapped, out_bias[None], residual
     )

time: 63.1 us -> 62.2 us (0.986)
  starting transfers between devices: 24.8 us -> 21.7 us
  waiting for transfers between devices: 22.7 us -> 24.4 us
  Pallas kernels: 12 us -> 13.2 us
  local copies, waits for them, and re-layouts: 1.65 us -> 0.94 us
    ppermute x2 -> x1, starting transfers between devices: 5.95 us -> 3.4 us  [to_partner(): lax.ppermute(block, 'rep', [(i, (i + count // 2) % count) for i in range(...]
    all_to_all x2, waiting for transfers between devices: 19.9 us -> 21.2 us  [exchange(): return lax.all_to_all(blocks, 'tp', 0, 0)]
    unnamed x17 -> x15, local copies, waits for them, and re-layouts: 1.65 us -> 0.94 us
    pallas_call x0 -> x1, Pallas kernels: none -> 0.68 us  [insert(): pl.pallas_call(insert_kernel, name='insert', compiler_params=pltpu.Compil...]
    ppermute x2 -> x1, waiting for transfers between devices: 2.79 us -> 3.19 us  [to_partner(): lax.ppermute(block, 'rep', [(i, (i + count // 2) % count) for i in range(...]
  transfers between devices with their start and end apart: 7 -> 6, of which waited for: 4 -> 3; matrix products, arithmetic and copies ran while one was open for 1% -> 1% of each run, Pallas kernels for 4% -> 6%
where the time goes in v4:
time: 62.2 us; the launch traced here: 61.7 us
  waiting for transfers between devices  24.4 us (39%)
  starting transfers between devices  21.7 us (35%)
  Pallas kernels  13.2 us (21%)
  between operations  1.44 us (2%)
  local copies, waits for them, and re-layouts  0.94 us (2%)
    all_to_all x2, waiting for transfers between devices, exchange(): return lax.all_to_all(blocks, 'tp', 0, 0)  21.2 us
    all_to_all x2, starting transfers between devices, exchange(): return lax.all_to_all(blocks, 'tp', 0, 0)  11 us
    ppermute x2, starting transfers between devices, to_pair(): lax.ppermute(block, 'tp', [(i, i ^ 2) for i in range(lax.axis_size('tp'))])  5.4 us
    pallas_call x1, Pallas kernels, decode(): pl.pallas_call(decode_kernel, name='decode', compiler_params=pltpu.Compil...  4.06 us
    pallas_call x1, Pallas kernels, project(): pl.pallas_call(project_kernel, name='project', compiler_params=pltpu.Comp...  3.66 us
    ppermute x1, starting transfers between devices, to_partner(): lax.ppermute(block, 'rep', [(i, (i + count // 2) % count) for i in range(...  3.4 us
    ppermute x1, waiting for transfers between devices, to_partner(): lax.ppermute(block, 'rep', [(i, (i + count // 2) % count) for i in range(...  3.19 us
    pallas_call x1, Pallas kernels, prompt(): pl.pallas_call(functools.partial(prompt_kernel, block=block), name='promp...  2.76 us
  transfers between devices with their start and end apart: 6, of which 3 were waited for; matrix products, arithmetic and copies ran while one was open for 1% of the time, Pallas kernels for 6%

profile of v4, /device:TPU:480, one launch (start us, length us, event | category | flops | bytes accessed | tf_op | source)
XLA Modules:
  0.0 61.7 jit_solution(9707545633859640668)
XLA Ops:
  0.6 0.0 copy-start.1
  0.6 0.0 copy-start.2
  0.7 0.0 copy-start.3
  0.7 4.1 %decode.1 = (bf16[1,2,264,256]{3,2,1,0:T(8,128)(2,1)}, bf16[1,256]{1,0:T(2,128)(2,1)S(1)}, bf16[1296,256]{1,0:T(8,128)(2,1)}) custom-call(s32[64]{0:T(128)} %moving_hbm.1, s32[128]{0:T(128)} %cache_len_hbm.1, bf16[2,256]{1,0:T(2,128)(2,1)} %new_q_hbm.1, bf16[2,256]{1,0:T(2,128)(2,1)} %new_k_hbm.1, bf16[2,256]{1,0:T(2,128)(2,1)} %new_v_hbm.1, ...), custom_call_target="tpu_custom_call" | custom-call | tf_op jit(solution)/shard_map/decode/pallas_call | solution.py:187
  4.7 3.5 %collective-permute-start.1 = (bf16[1296,256]{1,0:T(8,128)(2,1)}, bf16[1296,256]{1,0:T(8,128)(2,1)S(1)}, u32[]{:S(2)}, u32[]{:S(2)}) collective-permute-start(bf16[1296,256]{1,0:T(8,128)(2,1)} %get-tuple-element.13), channel_id=1, source_target_pairs={{0,2},{1,3},{2,0},{3,1},{4,6},{5,7},{6,4},{7,5},{8,10},{9,11},{10,... | collective-permute-start | bytes 1990664 | tf_op jit(solution)/shard_map/ppermute | solution.py:429
  8.2 3.4 %collective-permute-start = (bf16[1,2,264,256]{3,2,1,0:T(8,128)(2,1)}, bf16[1,2,264,256]{3,2,1,0:T(8,128)(2,1)S(1)}, u32[]{:S(2)}, u32[]{:S(2)}) collective-permute-start(bf16[1,2,264,256]{3,2,1,0:T(8,128)(2,1)} %get-tuple-element.12), channel_id=1, source_target_pairs={{0,256},{8,264},{16,272},{24,280},{32,288},{40,296},{48,304},{56,3... | collective-permute-start | bytes 811016 | tf_op jit(solution)/shard_map/ppermute | solution.py:425
  12.3 0.0 copy-done.1
  12.3 0.0 copy-done.2
  12.3 0.0 copy-done.3
  12.3 2.8 %prompt.1.given = bf16[8,264,256]{2,1,0:T(8,128)(2,1)} custom-call(s32[1]{0:T(128)S(6)} %copy.22.length_ref, bf16[512,256]{1,0:T(8,128)(2,1)S(1)} %copy-done.1, bf16[512,256]{1,0:T(8,128)(2,1)S(1)} %copy-done.2, bf16[512,256]{1,0:T(8,128)(2,1)S(1)} %copy-done.3), custom_call_target="tpu_custom_call" | custom-call | tf_op jit(solution)/shard_map/prompt/pallas_call | solution.py:252
  15.1 3.2 %collective-permute-done.come_ref = bf16[1,2,264,256]{3,2,1,0:T(8,128)(2,1)S(1)} collective-permute-done((bf16[1,2,264,256]{3,2,1,0:T(8,128)(2,1)}, bf16[1,2,264,256]{3,2,1,0:T(8,128)(2,1)S(1)}, u32[]{:S(2)}, u32[]{:S(2)}) %collective-permute-start) | collective-permute-done | bytes 270368 | tf_op jit(solution)/shard_map/ppermute | solution.py:425
  18.3 0.7 %insert.1 = bf16[8,264,256]{2,1,0:T(8,128)(2,1)} custom-call(bf16[1,256]{1,0:T(2,128)(2,1)S(1)} %get-tuple-element.11.stay_ref, bf16[1,2,264,256]{3,2,1,0:T(8,128)(2,1)S(1)} %collective-permute-done.come_ref, bf16[8,264,256]{2,1,0:T(8,128)(2,1)} %prompt.1.given), custom_call_target="tpu_custom_call", output_to_operand_aliasing={{}: (2, {})} | custom-call | tf_op jit(solution)/shard_map/insert/pallas_call | solution.py:285
  19.0 0.0 copy-start
  19.0 0.0 copy-start.4
  19.0 6.8 %all-to-all-start = ((bf16[8,264,256]{2,1,0:T(8,128)(2,1)}), bf16[8,264,256]{2,1,0:T(8,128)(2,1)S(1)}, u32[]{:S(2)}, u32[]{:S(2)}) async-start(bf16[8,264,256]{2,1,0:T(8,128)(2,1)} %insert.1), calls=%async_computation | async-start | bytes 2162688 | tf_op jit(solution)/shard_map/all_to_all | solution.py:437
  25.8 0.0 copy-start.5
  25.8 0.0 copy-start.6
  25.8 0.0 collective-permute-done.1.packed_ref
  25.8 1.9 %collective-permute-start.2 = (bf16[1296,256]{1,0:T(8,128)(2,1)S(1)}, bf16[1296,256]{1,0:T(8,128)(2,1)}, u32[]{:S(2)}, u32[]{:S(2)}) collective-permute-start(bf16[1296,256]{1,0:T(8,128)(2,1)S(1)} %collective-permute-done.1.packed_ref), channel_id=1, source_target_pairs={{0,8},{8,0},{16,24},{24,16},{32,40},{40,32},{48,56},{56,48},{64,72... | collective-permute-start | bytes 1990664 | tf_op jit(solution)/shard_map/ppermute | solution.py:433
  27.7 14.4 %all-to-all-done.x_ref = bf16[8,264,256]{2,1,0:T(8,128)(2,1)S(1)} async-done(((bf16[8,264,256]{2,1,0:T(8,128)(2,1)}), bf16[8,264,256]{2,1,0:T(8,128)(2,1)S(1)}, u32[]{:S(2)}, u32[]{:S(2)}) %all-to-all-start) | async-done | bytes 1081376 | tf_op jit(solution)/shard_map/all_to_all | solution.py:437
  42.1 0.0 collective-permute-done.2.swapped_ref
  42.1 0.0 copy-done
  42.1 0.0 copy-done.4
  42.1 3.7 %project.1 = (f32[264,256]{1,0:T(8,128)}, f32[264,256]{1,0:T(8,128)}, f32[8,2,264]{2,1,0:T(2,128)}) custom-call(bf16[8,264,256]{2,1,0:T(8,128)(2,1)S(1)} %all-to-all-done.x_ref, bf16[2048,256]{1,0:T(8,128)(2,1)S(1)} %copy-done, bf16[1296,256]{1,0:T(8,128)(2,1)S(1)} %collective-permute-done.1.packed_ref, ...), custom_call_target="tpu_custom_call" | custom-call | tf_op jit(solution)/shard_map/project/pallas_call | solution.py:352
  45.8 1.9 %collective-permute-start.3 = (f32[264,256]{1,0:T(8,128)}, f32[264,256]{1,0:T(8,128)S(1)}, u32[]{:S(2)}, u32[]{:S(2)}) collective-permute-start(f32[264,256]{1,0:T(8,128)} %get-tuple-element.16), channel_id=1, source_target_pairs={{0,2},{1,3},{2,0},{3,1},{4,6},{5,7},{6,4},{7,5},{8,10},{9,11},{10,... | collective-permute-start | bytes 811016 | tf_op jit(solution)/shard_map/ppermute | solution.py:429
  47.7 4.2 %all-to-all-start.1 = ((f32[8,2,264]{2,1,0:T(2,128)}), f32[8,2,264]{2,1,0:T(2,128)S(1)}, u32[]{:S(2)}, u32[]{:S(2)}) async-start(f32[8,2,264]{2,1,0:T(2,128)} %get-tuple-element.14), calls=%async_computation.1 | async-start | bytes 49152 | tf_op jit(solution)/shard_map/all_to_all | solution.py:437
  51.9 0.9 %copy.20 = bf16[1,2,260,256]{3,1,2,0:T(2,128)(2,1)} copy(bf16[1,2,260,256]{3,2,1,0:T(8,128)(2,1)S(1)} %bitcast.4) | data formatting | bytes 532480
  52.8 6.8 %all-to-all-done.1.stats_ref = f32[8,2,264]{2,1,0:T(2,128)S(1)} async-done(((f32[8,2,264]{2,1,0:T(2,128)}), f32[8,2,264]{2,1,0:T(2,128)S(1)}, u32[]{:S(2)}, u32[]{:S(2)}) %all-to-all-start.1) | async-done | bytes 16928 | tf_op jit(solution)/shard_map/all_to_all | solution.py:437
  59.7 0.0 collective-permute-done.3.come_ref
  59.7 0.0 copy-done.5
  59.7 0.0 copy-done.6
  59.7 2.0 %norm.1 = (bf16[514,256]{1,0:T(8,128)(2,1)}, bf16[514,256]{1,0:T(8,128)(2,1)}) custom-call(f32[8,2,264]{2,1,0:T(2,128)S(1)} %all-to-all-done.1.stats_ref, f32[264,256]{1,0:T(8,128)} %get-tuple-element.15.own_hbm, f32[264,256]{1,0:T(8,128)S(1)} %collective-permute-done.3.come_ref, f32[1,256]{1,0:T(1,128)S(1)} %bitcast.7, f32[1,256]{1,0:T(1,128)S(1)} %bitcast.8), custom_call_target="tpu_custom_call" | custom-call | tf_op jit(solution)/shard_map/norm/pallas_call | solution.py:412
Async XLA Ops:
  0.6 11.6 %copy-start.1 = (bf16[512,256]{1,0:T(8,128)(2,1)S(1)}, bf16[512,256]{1,0:T(8,128)(2,1)}, u32[]{:S(2)}) copy-start(bf16[512,256]{1,0:T(8,128)(2,1)} %q_ref.1) | copy-start | bytes 786436
  0.6 11.6 %copy-start.2 = (bf16[512,256]{1,0:T(8,128)(2,1)S(1)}, bf16[512,256]{1,0:T(8,128)(2,1)}, u32[]{:S(2)}) copy-start(bf16[512,256]{1,0:T(8,128)(2,1)} %k_ref.1) | copy-start | bytes 786436
  0.7 11.6 %copy-start.3 = (bf16[512,256]{1,0:T(8,128)(2,1)S(1)}, bf16[512,256]{1,0:T(8,128)(2,1)}, u32[]{:S(2)}) copy-start(bf16[512,256]{1,0:T(8,128)(2,1)} %v_ref.1) | copy-start | bytes 786436
  4.7 21.1 %collective-permute-start.1 = (bf16[1296,256]{1,0:T(8,128)(2,1)}, bf16[1296,256]{1,0:T(8,128)(2,1)S(1)}, u32[]{:S(2)}, u32[]{:S(2)}) collective-permute-start(bf16[1296,256]{1,0:T(8,128)(2,1)} %get-tuple-element.13), channel_id=1, source_target_pairs={{0,2},{1,3},{2,0},{3,1},{4,6},{5,7},{6,4},{7,5},{8,10},{9,11},{10,... | collective-permute-start | bytes 1990664 | tf_op jit(solution)/shard_map/ppermute | solution.py:429
  8.2 10.0 %collective-permute-start = (bf16[1,2,264,256]{3,2,1,0:T(8,128)(2,1)}, bf16[1,2,264,256]{3,2,1,0:T(8,128)(2,1)S(1)}, u32[]{:S(2)}, u32[]{:S(2)}) collective-permute-start(bf16[1,2,264,256]{3,2,1,0:T(8,128)(2,1)} %get-tuple-element.12), channel_id=1, source_target_pairs={{0,256},{8,264},{16,272},{24,280},{32,288},{40,296},{48,304},{56,3... | collective-permute-start | bytes 811016 | tf_op jit(solution)/shard_map/ppermute | solution.py:425
  19.0 23.2 %copy-start = (bf16[2048,256]{1,0:T(8,128)(2,1)S(1)}, bf16[2048,256]{1,0:T(8,128)(2,1)}, u32[]{:S(2)}) copy-start(bf16[2048,256]{1,0:T(8,128)(2,1)} %w_ref.1) | copy-start | bytes 3145732
  19.0 23.2 %copy-start.4 = (f32[256]{0:T(256)S(1)}, f32[256]{0:T(256)}, u32[]{:S(2)}) copy-start(f32[256]{0:T(256)} %param.28) | copy-start | bytes 3076
  19.0 23.1 %all-to-all-start = ((bf16[8,264,256]{2,1,0:T(8,128)(2,1)}), bf16[8,264,256]{2,1,0:T(8,128)(2,1)S(1)}, u32[]{:S(2)}, u32[]{:S(2)}) async-start(bf16[8,264,256]{2,1,0:T(8,128)(2,1)} %insert.1), calls=%async_computation | async-start | bytes 2162688 | tf_op jit(solution)/shard_map/all_to_all | solution.py:437
  25.8 33.9 %copy-start.5 = (f32[256]{0:T(256)S(1)}, f32[256]{0:T(256)}, u32[]{:S(2)}) copy-start(f32[256]{0:T(256)} %param.30) | copy-start | bytes 3076
  25.8 33.9 %copy-start.6 = (f32[256]{0:T(256)S(1)}, f32[256]{0:T(256)}, u32[]{:S(2)}) copy-start(f32[256]{0:T(256)} %param.31) | copy-start | bytes 3076
  25.8 16.3 %collective-permute-start.2 = (bf16[1296,256]{1,0:T(8,128)(2,1)S(1)}, bf16[1296,256]{1,0:T(8,128)(2,1)}, u32[]{:S(2)}, u32[]{:S(2)}) collective-permute-start(bf16[1296,256]{1,0:T(8,128)(2,1)S(1)} %collective-permute-done.1.packed_ref), channel_id=1, source_target_pairs={{0,8},{8,0},{16,24},{24,16},{32,40},{40,32},{48,56},{56,48},{64,72... | collective-permute-start | bytes 1990664 | tf_op jit(solution)/shard_map/ppermute | solution.py:433
  45.8 13.9 %collective-permute-start.3 = (f32[264,256]{1,0:T(8,128)}, f32[264,256]{1,0:T(8,128)S(1)}, u32[]{:S(2)}, u32[]{:S(2)}) collective-permute-start(f32[264,256]{1,0:T(8,128)} %get-tuple-element.16), channel_id=1, source_target_pairs={{0,2},{1,3},{2,0},{3,1},{4,6},{5,7},{6,4},{7,5},{8,10},{9,11},{10,... | collective-permute-start | bytes 811016 | tf_op jit(solution)/shard_map/ppermute | solution.py:429
  47.7 11.9 %all-to-all-start.1 = ((f32[8,2,264]{2,1,0:T(2,128)}), f32[8,2,264]{2,1,0:T(2,128)S(1)}, u32[]{:S(2)}, u32[]{:S(2)}) async-start(f32[8,2,264]{2,1,0:T(2,128)} %get-tuple-element.14), calls=%async_computation.1 | async-start | bytes 49152 | tf_op jit(solution)/shard_map/all_to_all | solution.py:437

commit v5 on v4

--- a/solution.py
+++ b/solution.py
@@ -369,16 +369,10 @@
     )(near(gathered), near(weight), near(packed), near(swapped), bias, far(residual))
 
 
-def norm_kernel(
-    stats_ref, own_hbm, come_ref, gain_ref, shift_ref, hidden_ref, normed_ref, own_ref, sem,
-):
-    copy = pltpu.make_async_copy(own_hbm, own_ref, sem)
-    copy.start()
-    members = stats_ref.shape[0]
-    rows, width = own_ref.shape
+def tables_kernel(stats_ref, out_ref, *, width):
+    members, _, rows = stats_ref.shape
     parts = members // 2
-    side = side_of()
-    tables = []
+    row = lax.broadcasted_iota(jnp.int32, (8, rows), 0)
     for half in range(2):
         sources = [s for s in range(members) if s // 2 % 2 == half]
         means = [stats_ref[s, 0:1, :] for s in sources]
@@ -388,16 +382,36 @@
             for s, part in zip(sources, means)
         )
         scale = lax.rsqrt(spread * (1.0 / (members * width)) + EPSILON)
-        row = lax.broadcasted_iota(jnp.int32, (8, rows), 0)
-        tables.append(jnp.where(row == 0, mean, jnp.where(row == 1, scale, 0.0)))
+        out_ref[half] = jnp.where(row == 0, mean, jnp.where(row == 1, scale, 0.0))
+
+
+def tables(stats, width):
+    return pl.pallas_call(
+        functools.partial(tables_kernel, width=width),
+        name="tables",
+        cost_estimate=pl.CostEstimate(flops=8 * 10**9, bytes_accessed=2**20, transcendentals=0),
+        compiler_params=pltpu.CompilerParams(vmem_limit_bytes=ROOM),
+        out_shape=kept((2, 8, stats.shape[2]), F32),
+        in_specs=[VMEM],
+        out_specs=VMEM,
+    )(near(stats))
+
+
+def norm_kernel(
+    tables_ref, own_hbm, come_ref, gain_ref, shift_ref, hidden_ref, normed_ref, own_ref, sem,
+):
+    copy = pltpu.make_async_copy(own_hbm, own_ref, sem)
+    copy.start()
     copy.wait()
+    rows, width = own_ref.shape
+    side = side_of()
     total = hidden_ref.shape[0]
-    for half, table in enumerate(tables):
+    for half in range(2):
         first = half * (rows - 8)
         used = rows - 8 if half == 0 else total - first
         for start in range(0, used, BLOCK):
             at = slice(start, min(start + BLOCK, used))
-            columns = table[:, at].T
+            columns = tables_ref[half, :, at].T
             own, come = own_ref[at], come_ref[at]
             stream = jnp.where(side == half, own, come)
             to = slice(first + at.start, first + at.stop)
@@ -407,7 +421,7 @@
             ).astype(BF16)
 
 
-def norm(stats, own, come, gain, shift, rows):
+def norm(scales, own, come, gain, shift, rows):
     out = jax.ShapeDtypeStruct((rows, own.shape[1]), BF16)
     return pl.pallas_call(
         norm_kernel,
@@ -417,7 +431,7 @@
         in_specs=[VMEM, HBM, VMEM, VMEM, VMEM],
         out_specs=(VMEM, VMEM),
         scratch_shapes=[pltpu.VMEM(own.shape, F32), pltpu.SemaphoreType.DMA],
-    )(near(stats), far(own), near(come), gain, shift)
+    )(near(scales), far(own), near(come), gain, shift)
 
 
 def to_partner(block):
@@ -457,9 +471,9 @@
     own, pair, stats = project(
         exchange(mixed), out_weight, packed, swapped, out_bias[None], residual
     )
-    stats = exchange(stats)
+    scales = tables(exchange(stats), own.shape[1])
     hidden_out, normed = norm(
-        stats, own, to_pair(pair), ln_gain[None], ln_shift[None], residual.shape[0]
+        scales, own, to_pair(pair), ln_gain[None], ln_shift[None], residual.shape[0]
     )
     return (hidden_out, normed, moved_window)
 

time: 62.2 us -> 61.7 us (level)
  waiting for transfers between devices: 24.4 us -> 22.3 us
  starting transfers between devices: 21.7 us -> 22.9 us
    all_to_all x2, waiting for transfers between devices: 21.2 us -> 17.3 us  [exchange(): return lax.all_to_all(blocks, 'tp', 0, 0)]
    ppermute x2, starting transfers between devices: 5.4 us -> 7.44 us  [to_pair(): lax.ppermute(block, 'tp', [(i, i ^ 2) for i in range(lax.axis_size('tp'))])]
    ppermute x2, waiting for transfers between devices: 0.01 us -> 1.82 us  [to_pair(): lax.ppermute(block, 'tp', [(i, i ^ 2) for i in range(lax.axis_size('tp'))])]
    all_to_all x2, starting transfers between devices: 11 us -> 10.1 us  [exchange(): return lax.all_to_all(blocks, 'tp', 0, 0)]
  transfers between devices with their start and end apart: 6 -> 6, of which waited for: 3 -> 4; matrix products, arithmetic and copies ran while one was open for 1% -> 1% of each run, Pallas kernels for 6% -> 6%
where the time goes in v5:
time: 61.7 us; the launch traced here: 60.8 us
  starting transfers between devices  22.9 us (37%)
  waiting for transfers between devices  22.3 us (36%)
  Pallas kernels  13.2 us (21%)
  between operations  1.43 us (2%)
  local copies, waits for them, and re-layouts  0.94 us (2%)
    all_to_all x2, waiting for transfers between devices, exchange(): return lax.all_to_all(blocks, 'tp', 0, 0)  17.3 us
    all_to_all x2, starting transfers between devices, exchange(): return lax.all_to_all(blocks, 'tp', 0, 0)  10.1 us
    ppermute x2, starting transfers between devices, to_pair(): lax.ppermute(block, 'tp', [(i, i ^ 2) for i in range(lax.axis_size('tp'))])  7.44 us
    pallas_call x1, Pallas kernels, decode(): pl.pallas_call(decode_kernel, name='decode', compiler_params=pltpu.Compil...  4.06 us
    pallas_call x1, Pallas kernels, project(): pl.pallas_call(project_kernel, name='project', compiler_params=pltpu.Comp...  3.66 us
    ppermute x1, starting transfers between devices, to_partner(): lax.ppermute(block, 'rep', [(i, (i + count // 2) % count) for i in range(...  3.4 us
    ppermute x1, waiting for transfers between devices, to_partner(): lax.ppermute(block, 'rep', [(i, (i + count // 2) % count) for i in range(...  3.18 us
    pallas_call x1, Pallas kernels, prompt(): pl.pallas_call(functools.partial(prompt_kernel, block=block), name='promp...  2.78 us
  transfers between devices with their start and end apart: 6, of which 4 were waited for; matrix products, arithmetic and copies ran while one was open for 1% of the time, Pallas kernels for 6%

profile of v5, /device:TPU:480, one launch (start us, length us, event | category | flops | bytes accessed | tf_op | source)
XLA Modules:
  0.0 60.8 jit_solution(11917873172936221301)
XLA Ops:
  0.6 0.0 copy-start.1
  0.6 0.0 copy-start.2
  0.7 0.0 copy-start.3
  0.7 4.1 %decode.1 = (bf16[1,2,264,256]{3,2,1,0:T(8,128)(2,1)}, bf16[1,256]{1,0:T(2,128)(2,1)S(1)}, bf16[1296,256]{1,0:T(8,128)(2,1)}) custom-call(s32[64]{0:T(128)} %moving_hbm.1, s32[128]{0:T(128)} %cache_len_hbm.1, bf16[2,256]{1,0:T(2,128)(2,1)} %new_q_hbm.1, bf16[2,256]{1,0:T(2,128)(2,1)} %new_k_hbm.1, bf16[2,256]{1,0:T(2,128)(2,1)} %new_v_hbm.1, ...), custom_call_target="tpu_custom_call" | custom-call | tf_op jit(solution)/shard_map/decode/pallas_call | solution.py:187
  4.7 3.5 %collective-permute-start.1 = (bf16[1296,256]{1,0:T(8,128)(2,1)}, bf16[1296,256]{1,0:T(8,128)(2,1)S(1)}, u32[]{:S(2)}, u32[]{:S(2)}) collective-permute-start(bf16[1296,256]{1,0:T(8,128)(2,1)} %get-tuple-element.13), channel_id=1, source_target_pairs={{0,2},{1,3},{2,0},{3,1},{4,6},{5,7},{6,4},{7,5},{8,10},{9,11},{10,... | collective-permute-start | bytes 1990664 | tf_op jit(solution)/shard_map/ppermute | solution.py:443
  8.2 3.4 %collective-permute-start = (bf16[1,2,264,256]{3,2,1,0:T(8,128)(2,1)}, bf16[1,2,264,256]{3,2,1,0:T(8,128)(2,1)S(1)}, u32[]{:S(2)}, u32[]{:S(2)}) collective-permute-start(bf16[1,2,264,256]{3,2,1,0:T(8,128)(2,1)} %get-tuple-element.12), channel_id=1, source_target_pairs={{0,256},{8,264},{16,272},{24,280},{32,288},{40,296},{48,304},{56,3... | collective-permute-start | bytes 811016 | tf_op jit(solution)/shard_map/ppermute | solution.py:439
  12.3 0.0 copy-done.1
  12.3 0.0 copy-done.2
  12.3 0.0 copy-done.3
  12.3 2.8 %prompt.1.given = bf16[8,264,256]{2,1,0:T(8,128)(2,1)} custom-call(s32[1]{0:T(128)S(6)} %copy.22.length_ref, bf16[512,256]{1,0:T(8,128)(2,1)S(1)} %copy-done.1, bf16[512,256]{1,0:T(8,128)(2,1)S(1)} %copy-done.2, bf16[512,256]{1,0:T(8,128)(2,1)S(1)} %copy-done.3), custom_call_target="tpu_custom_call" | custom-call | tf_op jit(solution)/shard_map/prompt/pallas_call | solution.py:252
  15.1 3.2 %collective-permute-done.come_ref = bf16[1,2,264,256]{3,2,1,0:T(8,128)(2,1)S(1)} collective-permute-done((bf16[1,2,264,256]{3,2,1,0:T(8,128)(2,1)}, bf16[1,2,264,256]{3,2,1,0:T(8,128)(2,1)S(1)}, u32[]{:S(2)}, u32[]{:S(2)}) %collective-permute-start) | collective-permute-done | bytes 270368 | tf_op jit(solution)/shard_map/ppermute | solution.py:439
  18.3 0.7 %insert.1 = bf16[8,264,256]{2,1,0:T(8,128)(2,1)} custom-call(bf16[1,256]{1,0:T(2,128)(2,1)S(1)} %get-tuple-element.11.stay_ref, bf16[1,2,264,256]{3,2,1,0:T(8,128)(2,1)S(1)} %collective-permute-done.come_ref, bf16[8,264,256]{2,1,0:T(8,128)(2,1)} %prompt.1.given), custom_call_target="tpu_custom_call", output_to_operand_aliasing={{}: (2, {})} | custom-call | tf_op jit(solution)/shard_map/insert/pallas_call | solution.py:285
  19.0 0.0 copy-start
  19.0 0.0 copy-start.4
  19.0 6.8 %all-to-all-start = ((bf16[8,264,256]{2,1,0:T(8,128)(2,1)}), bf16[8,264,256]{2,1,0:T(8,128)(2,1)S(1)}, u32[]{:S(2)}, u32[]{:S(2)}) async-start(bf16[8,264,256]{2,1,0:T(8,128)(2,1)} %insert.1), calls=%async_computation | async-start | bytes 2162688 | tf_op jit(solution)/shard_map/all_to_all | solution.py:451
  25.8 0.0 collective-permute-done.1.packed_ref
  25.8 1.9 %collective-permute-start.2 = (bf16[1296,256]{1,0:T(8,128)(2,1)S(1)}, bf16[1296,256]{1,0:T(8,128)(2,1)}, u32[]{:S(2)}, u32[]{:S(2)}) collective-permute-start(bf16[1296,256]{1,0:T(8,128)(2,1)S(1)} %collective-permute-done.1.packed_ref), channel_id=1, source_target_pairs={{0,8},{8,0},{16,24},{24,16},{32,40},{40,32},{48,56},{56,48},{64,72... | collective-permute-start | bytes 1990664 | tf_op jit(solution)/shard_map/ppermute | solution.py:447
  27.7 14.4 %all-to-all-done.x_ref = bf16[8,264,256]{2,1,0:T(8,128)(2,1)S(1)} async-done(((bf16[8,264,256]{2,1,0:T(8,128)(2,1)}), bf16[8,264,256]{2,1,0:T(8,128)(2,1)S(1)}, u32[]{:S(2)}, u32[]{:S(2)}) %all-to-all-start) | async-done | bytes 1081376 | tf_op jit(solution)/shard_map/all_to_all | solution.py:451
  42.1 0.0 collective-permute-done.2.swapped_ref
  42.1 0.0 copy-done
  42.1 0.0 copy-done.4
  42.1 3.7 %project.1 = (f32[264,256]{1,0:T(8,128)}, f32[264,256]{1,0:T(8,128)}, f32[8,2,264]{2,1,0:T(2,128)}) custom-call(bf16[8,264,256]{2,1,0:T(8,128)(2,1)S(1)} %all-to-all-done.x_ref, bf16[2048,256]{1,0:T(8,128)(2,1)S(1)} %copy-done, bf16[1296,256]{1,0:T(8,128)(2,1)S(1)} %collective-permute-done.1.packed_ref, ...), custom_call_target="tpu_custom_call" | custom-call | tf_op jit(solution)/shard_map/project/pallas_call | solution.py:352
  45.8 3.4 %all-to-all-start.1 = ((f32[8,2,264]{2,1,0:T(2,128)}), f32[8,2,264]{2,1,0:T(2,128)S(1)}, u32[]{:S(2)}, u32[]{:S(2)}) async-start(f32[8,2,264]{2,1,0:T(2,128)} %get-tuple-element.14), calls=%async_computation.1 | async-start | bytes 49152 | tf_op jit(solution)/shard_map/all_to_all | solution.py:451
  49.2 0.9 %copy.20 = bf16[1,2,260,256]{3,1,2,0:T(2,128)(2,1)} copy(bf16[1,2,260,256]{3,2,1,0:T(8,128)(2,1)S(1)} %bitcast.4) | data formatting | bytes 532480
  50.1 0.0 copy-start.5
  50.1 0.0 copy-start.6
  50.1 4.0 %collective-permute-start.3 = (f32[264,256]{1,0:T(8,128)}, f32[264,256]{1,0:T(8,128)S(1)}, u32[]{:S(2)}, u32[]{:S(2)}) collective-permute-start(f32[264,256]{1,0:T(8,128)} %get-tuple-element.16), channel_id=1, source_target_pairs={{0,2},{1,3},{2,0},{3,1},{4,6},{5,7},{6,4},{7,5},{8,10},{9,11},{10,... | collective-permute-start | bytes 811016 | tf_op jit(solution)/shard_map/ppermute | solution.py:443
  54.0 2.9 %all-to-all-done.1.stats_ref = f32[8,2,264]{2,1,0:T(2,128)S(1)} async-done(((f32[8,2,264]{2,1,0:T(2,128)}), f32[8,2,264]{2,1,0:T(2,128)S(1)}, u32[]{:S(2)}, u32[]{:S(2)}) %all-to-all-start.1) | async-done | bytes 16928 | tf_op jit(solution)/shard_map/all_to_all | solution.py:451
  57.0 1.8 %collective-permute-done.3.come_ref = f32[264,256]{1,0:T(8,128)S(1)} collective-permute-done((f32[264,256]{1,0:T(8,128)}, f32[264,256]{1,0:T(8,128)S(1)}, u32[]{:S(2)}, u32[]{:S(2)}) %collective-permute-start.3) | collective-permute-done | bytes 270368 | tf_op jit(solution)/shard_map/ppermute | solution.py:443
  58.8 0.0 copy-done.5
  58.8 0.0 copy-done.6
  58.8 2.0 %norm.1 = (bf16[514,256]{1,0:T(8,128)(2,1)}, bf16[514,256]{1,0:T(8,128)(2,1)}) custom-call(f32[2,8,264]{2,1,0:T(8,128)S(1)} %tables.1.tables_ref, f32[264,256]{1,0:T(8,128)} %get-tuple-element.15.own_hbm, f32[264,256]{1,0:T(8,128)S(1)} %collective-permute-done.3.come_ref, f32[1,256]{1,0:T(1,128)S(1)} %bitcast.7, f32[1,256]{1,0:T(1,128)S(1)} %bitcast.8), custom_call_target="tpu_custom_call" | custom-call | tf_op jit(solution)/shard_map/norm/pallas_call | solution.py:426
  (1 shorter events, 0.0 us)
Async XLA Ops:
  0.6 11.6 %copy-start.1 = (bf16[512,256]{1,0:T(8,128)(2,1)S(1)}, bf16[512,256]{1,0:T(8,128)(2,1)}, u32[]{:S(2)}) copy-start(bf16[512,256]{1,0:T(8,128)(2,1)} %q_ref.1) | copy-start | bytes 786436
  0.6 11.6 %copy-start.2 = (bf16[512,256]{1,0:T(8,128)(2,1)S(1)}, bf16[512,256]{1,0:T(8,128)(2,1)}, u32[]{:S(2)}) copy-start(bf16[512,256]{1,0:T(8,128)(2,1)} %k_ref.1) | copy-start | bytes 786436
  0.7 11.6 %copy-start.3 = (bf16[512,256]{1,0:T(8,128)(2,1)S(1)}, bf16[512,256]{1,0:T(8,128)(2,1)}, u32[]{:S(2)}) copy-start(bf16[512,256]{1,0:T(8,128)(2,1)} %v_ref.1) | copy-start | bytes 786436
  4.7 21.0 %collective-permute-start.1 = (bf16[1296,256]{1,0:T(8,128)(2,1)}, bf16[1296,256]{1,0:T(8,128)(2,1)S(1)}, u32[]{:S(2)}, u32[]{:S(2)}) collective-permute-start(bf16[1296,256]{1,0:T(8,128)(2,1)} %get-tuple-element.13), channel_id=1, source_target_pairs={{0,2},{1,3},{2,0},{3,1},{4,6},{5,7},{6,4},{7,5},{8,10},{9,11},{10,... | collective-permute-start | bytes 1990664 | tf_op jit(solution)/shard_map/ppermute | solution.py:443
  8.2 10.0 %collective-permute-start = (bf16[1,2,264,256]{3,2,1,0:T(8,128)(2,1)}, bf16[1,2,264,256]{3,2,1,0:T(8,128)(2,1)S(1)}, u32[]{:S(2)}, u32[]{:S(2)}) collective-permute-start(bf16[1,2,264,256]{3,2,1,0:T(8,128)(2,1)} %get-tuple-element.12), channel_id=1, source_target_pairs={{0,256},{8,264},{16,272},{24,280},{32,288},{40,296},{48,304},{56,3... | collective-permute-start | bytes 811016 | tf_op jit(solution)/shard_map/ppermute | solution.py:439
  19.0 23.2 %copy-start = (bf16[2048,256]{1,0:T(8,128)(2,1)S(1)}, bf16[2048,256]{1,0:T(8,128)(2,1)}, u32[]{:S(2)}) copy-start(bf16[2048,256]{1,0:T(8,128)(2,1)} %w_ref.1) | copy-start | bytes 3145732
  19.0 23.2 %copy-start.4 = (f32[256]{0:T(256)S(1)}, f32[256]{0:T(256)}, u32[]{:S(2)}) copy-start(f32[256]{0:T(256)} %param.28) | copy-start | bytes 3076
  19.0 23.1 %all-to-all-start = ((bf16[8,264,256]{2,1,0:T(8,128)(2,1)}), bf16[8,264,256]{2,1,0:T(8,128)(2,1)S(1)}, u32[]{:S(2)}, u32[]{:S(2)}) async-start(bf16[8,264,256]{2,1,0:T(8,128)(2,1)} %insert.1), calls=%async_computation | async-start | bytes 2162688 | tf_op jit(solution)/shard_map/all_to_all | solution.py:451
  25.8 16.4 %collective-permute-start.2 = (bf16[1296,256]{1,0:T(8,128)(2,1)S(1)}, bf16[1296,256]{1,0:T(8,128)(2,1)}, u32[]{:S(2)}, u32[]{:S(2)}) collective-permute-start(bf16[1296,256]{1,0:T(8,128)(2,1)S(1)} %collective-permute-done.1.packed_ref), channel_id=1, source_target_pairs={{0,8},{8,0},{16,24},{24,16},{32,40},{40,32},{48,56},{56,48},{64,72... | collective-permute-start | bytes 1990664 | tf_op jit(solution)/shard_map/ppermute | solution.py:447
  45.8 11.1 %all-to-all-start.1 = ((f32[8,2,264]{2,1,0:T(2,128)}), f32[8,2,264]{2,1,0:T(2,128)S(1)}, u32[]{:S(2)}, u32[]{:S(2)}) async-start(f32[8,2,264]{2,1,0:T(2,128)} %get-tuple-element.14), calls=%async_computation.1 | async-start | bytes 49152 | tf_op jit(solution)/shard_map/all_to_all | solution.py:451
  50.1 8.7 %copy-start.5 = (f32[256]{0:T(256)S(1)}, f32[256]{0:T(256)}, u32[]{:S(2)}) copy-start(f32[256]{0:T(256)} %param.30) | copy-start | bytes 3076
  50.1 8.7 %copy-start.6 = (f32[256]{0:T(256)S(1)}, f32[256]{0:T(256)}, u32[]{:S(2)}) copy-start(f32[256]{0:T(256)} %param.31) | copy-start | bytes 3076
  50.1 8.7 %collective-permute-start.3 = (f32[264,256]{1,0:T(8,128)}, f32[264,256]{1,0:T(8,128)S(1)}, u32[]{:S(2)}, u32[]{:S(2)}) collective-permute-start(f32[264,256]{1,0:T(8,128)} %get-tuple-element.16), channel_id=1, source_target_pairs={{0,2},{1,3},{2,0},{3,1},{4,6},{5,7},{6,4},{7,5},{8,10},{9,11},{10,... | collective-permute-start | bytes 811016 | tf_op jit(solution)/shard_map/ppermute | solution.py:443

commit v6 on v5

--- a/solution.py
+++ b/solution.py
@@ -5,6 +5,7 @@
 import jax.numpy as jnp
 from jax import lax
 from jax.experimental import pallas as pl
+from jax.experimental.layout import Layout, with_layout_constraint
 from jax.experimental.pallas import tpu as pltpu
 from jax.sharding import PartitionSpec as P
 
@@ -462,14 +463,16 @@
     window, stay_row, packed = decode(
         moving, cache_len, new_q, new_k, new_v, cache_keys, cache_values, out_weight, residual, out_bias[None]
     )
-    come = to_partner(window)
+    come = with_layout_constraint(to_partner(window), Layout((0, 1, 2, 3)))
     packed = to_pair(packed)
     swapped = to_sibling(packed)
     mixed = prompt(prompt_len, prompt_q, prompt_k, prompt_v, lax.axis_size("tp"))
     mixed = insert(stay_row, come, mixed)
-    moved_window = come[:, :, :SPAN]
+    by_row = with_layout_constraint(jnp.transpose(come[:, :, :SPAN], (0, 2, 1, 3)), Layout((0, 1, 2, 3)))
+    gathered, by_row = lax.optimization_barrier((exchange(mixed), by_row))
+    moved_window = jnp.transpose(by_row, (0, 2, 1, 3))
     own, pair, stats = project(
-        exchange(mixed), out_weight, packed, swapped, out_bias[None], residual
+        gathered, out_weight, packed, swapped, out_bias[None], residual
     )
     scales = tables(exchange(stats), own.shape[1])
     hidden_out, normed = norm(

time: 61.7 us -> 60.8 us (0.985)
  waiting for transfers between devices: 22.3 us -> 21.5 us
    ppermute x2, waiting for transfers between devices: 1.82 us -> 1.04 us  [to_pair(): lax.ppermute(block, 'tp', [(i, i ^ 2) for i in range(lax.axis_size('tp'))])]
  transfers between devices with their start and end apart: 6 -> 6, of which waited for: 4 -> 4; matrix products, arithmetic and copies ran while one was open for 1% -> 2% of each run, Pallas kernels for 6% -> 6%
where the time goes in v6:
time: 60.8 us; the launch traced here: 60 us
  starting transfers between devices  22.9 us (38%)
  waiting for transfers between devices  21.5 us (35%)
  Pallas kernels  13.2 us (22%)
  between operations  1.45 us (2%)
  local copies, waits for them, and re-layouts  0.95 us (2%)
    all_to_all x2, waiting for transfers between devices, exchange(): return lax.all_to_all(blocks, 'tp', 0, 0)  17.3 us
    all_to_all x2, starting transfers between devices, exchange(): return lax.all_to_all(blocks, 'tp', 0, 0)  10.1 us
    ppermute x2, starting transfers between devices, to_pair(): lax.ppermute(block, 'tp', [(i, i ^ 2) for i in range(lax.axis_size('tp'))])  7.42 us
    pallas_call x1, Pallas kernels, decode(): pl.pallas_call(decode_kernel, name='decode', compiler_params=pltpu.Compil...  4.06 us
    pallas_call x1, Pallas kernels, project(): pl.pallas_call(project_kernel, name='project', compiler_params=pltpu.Comp...  3.65 us
    ppermute x1, starting transfers between devices, to_partner(): lax.ppermute(block, 'rep', [(i, (i + count // 2) % count) for i in range(...  3.4 us
    ppermute x1, waiting for transfers between devices, to_partner(): lax.ppermute(block, 'rep', [(i, (i + count // 2) % count) for i in range(...  3.18 us
    pallas_call x1, Pallas kernels, prompt(): pl.pallas_call(functools.partial(prompt_kernel, block=block), name='promp...  2.78 us
  transfers between devices with their start and end apart: 6, of which 4 were waited for; matrix products, arithmetic and copies ran while one was open for 2% of the time, Pallas kernels for 6%

profile of v6, /device:TPU:480, one launch (start us, length us, event | category | flops | bytes accessed | tf_op | source)
XLA Modules:
  0.0 60.0 jit_solution(13370356341133795671)
XLA Ops:
  0.6 0.0 copy-start.1
  0.6 0.0 copy-start.2
  0.7 0.0 copy-start.3
  0.7 4.1 %decode.1 = (bf16[1,2,264,256]{3,2,1,0:T(8,128)(2,1)}, bf16[1,256]{1,0:T(2,128)(2,1)S(1)}, bf16[1296,256]{1,0:T(8,128)(2,1)}) custom-call(s32[64]{0:T(128)} %moving_hbm.1, s32[128]{0:T(128)} %cache_len_hbm.1, bf16[2,256]{1,0:T(2,128)(2,1)} %new_q_hbm.1, bf16[2,256]{1,0:T(2,128)(2,1)} %new_k_hbm.1, bf16[2,256]{1,0:T(2,128)(2,1)} %new_v_hbm.1, ...), custom_call_target="tpu_custom_call" | custom-call | tf_op jit(solution)/shard_map/decode/pallas_call | solution.py:188
  4.7 3.5 %collective-permute-start.1 = (bf16[1296,256]{1,0:T(8,128)(2,1)}, bf16[1296,256]{1,0:T(8,128)(2,1)S(1)}, u32[]{:S(2)}, u32[]{:S(2)}) collective-permute-start(bf16[1296,256]{1,0:T(8,128)(2,1)} %get-tuple-element.16), channel_id=1, source_target_pairs={{0,2},{1,3},{2,0},{3,1},{4,6},{5,7},{6,4},{7,5},{8,10},{9,11},{10,... | collective-permute-start | bytes 1990664 | tf_op jit(solution)/shard_map/ppermute | solution.py:444
  8.2 3.4 %collective-permute-start = (bf16[1,2,264,256]{3,2,1,0:T(8,128)(2,1)}, bf16[1,2,264,256]{3,2,1,0:T(8,128)(2,1)S(1)}, u32[]{:S(2)}, u32[]{:S(2)}) collective-permute-start(bf16[1,2,264,256]{3,2,1,0:T(8,128)(2,1)} %get-tuple-element.14), channel_id=1, source_target_pairs={{0,256},{8,264},{16,272},{24,280},{32,288},{40,296},{48,304},{56,3... | collective-permute-start | bytes 811016 | tf_op jit(solution)/shard_map/ppermute | solution.py:440
  12.3 0.0 copy-done.1
  12.3 0.0 copy-done.2
  12.3 0.0 copy-done.3
  12.3 2.8 %prompt.1.given = bf16[8,264,256]{2,1,0:T(8,128)(2,1)} custom-call(s32[1]{0:T(128)S(6)} %copy.25.length_ref, bf16[512,256]{1,0:T(8,128)(2,1)S(1)} %copy-done.1, bf16[512,256]{1,0:T(8,128)(2,1)S(1)} %copy-done.2, bf16[512,256]{1,0:T(8,128)(2,1)S(1)} %copy-done.3), custom_call_target="tpu_custom_call" | custom-call | tf_op jit(solution)/shard_map/prompt/pallas_call | solution.py:253
  15.1 3.2 %collective-permute-done.come_ref = bf16[1,2,264,256]{3,2,1,0:T(8,128)(2,1)S(1)} collective-permute-done((bf16[1,2,264,256]{3,2,1,0:T(8,128)(2,1)}, bf16[1,2,264,256]{3,2,1,0:T(8,128)(2,1)S(1)}, u32[]{:S(2)}, u32[]{:S(2)}) %collective-permute-start) | collective-permute-done | bytes 270368 | tf_op jit(solution)/shard_map/ppermute | solution.py:440
  18.3 0.7 %insert.1 = bf16[8,264,256]{2,1,0:T(8,128)(2,1)} custom-call(bf16[1,256]{1,0:T(2,128)(2,1)S(1)} %get-tuple-element.13.stay_ref, bf16[1,2,264,256]{3,2,1,0:T(8,128)(2,1)S(1)} %collective-permute-done.come_ref, bf16[8,264,256]{2,1,0:T(8,128)(2,1)} %prompt.1.given), custom_call_target="tpu_custom_call", output_to_operand_aliasing={{}: (2, {})} | custom-call | tf_op jit(solution)/shard_map/insert/pallas_call | solution.py:286
  19.0 0.0 copy-start
  19.0 0.0 copy-start.4
  19.0 6.8 %all-to-all-start = ((bf16[8,264,256]{2,1,0:T(8,128)(2,1)}), bf16[8,264,256]{2,1,0:T(8,128)(2,1)S(1)}, u32[]{:S(2)}, u32[]{:S(2)}) async-start(bf16[8,264,256]{2,1,0:T(8,128)(2,1)} %insert.1), calls=%async_computation | async-start | bytes 2162688 | tf_op jit(solution)/shard_map/all_to_all | solution.py:452
  25.8 0.0 collective-permute-done.1.packed_ref
  25.8 1.9 %collective-permute-start.2 = (bf16[1296,256]{1,0:T(8,128)(2,1)S(1)}, bf16[1296,256]{1,0:T(8,128)(2,1)}, u32[]{:S(2)}, u32[]{:S(2)}) collective-permute-start(bf16[1296,256]{1,0:T(8,128)(2,1)S(1)} %collective-permute-done.1.packed_ref), channel_id=1, source_target_pairs={{0,8},{8,0},{16,24},{24,16},{32,40},{40,32},{48,56},{56,48},{64,72... | collective-permute-start | bytes 1990664 | tf_op jit(solution)/shard_map/ppermute | solution.py:448
  27.7 0.9 %copy.23 = bf16[1,2,260,256]{3,1,2,0:T(2,128)(2,1)} copy(bf16[1,2,260,256]{3,2,1,0:T(8,128)(2,1)S(1)} %bitcast.8) | data formatting | bytes 532480
  28.6 13.5 %all-to-all-done.x_ref = bf16[8,264,256]{2,1,0:T(8,128)(2,1)S(1)} async-done(((bf16[8,264,256]{2,1,0:T(8,128)(2,1)}), bf16[8,264,256]{2,1,0:T(8,128)(2,1)S(1)}, u32[]{:S(2)}, u32[]{:S(2)}) %all-to-all-start) | async-done | bytes 1081376 | tf_op jit(solution)/shard_map/all_to_all | solution.py:452
  42.1 0.0 collective-permute-done.2.swapped_ref
  42.1 0.0 copy-done
  42.1 0.0 copy-done.4
  42.1 3.6 %project.1 = (f32[264,256]{1,0:T(8,128)}, f32[264,256]{1,0:T(8,128)}, f32[8,2,264]{2,1,0:T(2,128)}) custom-call(bf16[8,264,256]{2,1,0:T(8,128)(2,1)S(1)} %all-to-all-done.x_ref, bf16[2048,256]{1,0:T(8,128)(2,1)S(1)} %copy-done, bf16[1296,256]{1,0:T(8,128)(2,1)S(1)} %collective-permute-done.1.packed_ref, ...), custom_call_target="tpu_custom_call" | custom-call | tf_op jit(solution)/shard_map/project/pallas_call | solution.py:353
  45.8 3.4 %all-to-all-start.1 = ((f32[8,2,264]{2,1,0:T(2,128)}), f32[8,2,264]{2,1,0:T(2,128)S(1)}, u32[]{:S(2)}, u32[]{:S(2)}) async-start(f32[8,2,264]{2,1,0:T(2,128)} %get-tuple-element.17), calls=%async_computation.1 | async-start | bytes 49152 | tf_op jit(solution)/shard_map/all_to_all | solution.py:452
  49.2 0.0 copy-start.5
  49.2 0.0 copy-start.6
  49.2 3.9 %collective-permute-start.3 = (f32[264,256]{1,0:T(8,128)}, f32[264,256]{1,0:T(8,128)S(1)}, u32[]{:S(2)}, u32[]{:S(2)}) collective-permute-start(f32[264,256]{1,0:T(8,128)} %get-tuple-element.19), channel_id=1, source_target_pairs={{0,2},{1,3},{2,0},{3,1},{4,6},{5,7},{6,4},{7,5},{8,10},{9,11},{10,... | collective-permute-start | bytes 811016 | tf_op jit(solution)/shard_map/ppermute | solution.py:444
  53.1 3.8 %all-to-all-done.1.stats_ref = f32[8,2,264]{2,1,0:T(2,128)S(1)} async-done(((f32[8,2,264]{2,1,0:T(2,128)}), f32[8,2,264]{2,1,0:T(2,128)S(1)}, u32[]{:S(2)}, u32[]{:S(2)}) %all-to-all-start.1) | async-done | bytes 16928 | tf_op jit(solution)/shard_map/all_to_all | solution.py:452
  56.9 1.0 %collective-permute-done.3.come_ref = f32[264,256]{1,0:T(8,128)S(1)} collective-permute-done((f32[264,256]{1,0:T(8,128)}, f32[264,256]{1,0:T(8,128)S(1)}, u32[]{:S(2)}, u32[]{:S(2)}) %collective-permute-start.3) | collective-permute-done | bytes 270368 | tf_op jit(solution)/shard_map/ppermute | solution.py:444
  58.0 0.0 copy-done.5
  58.0 0.0 copy-done.6
  58.0 2.0 %norm.1 = (bf16[514,256]{1,0:T(8,128)(2,1)}, bf16[514,256]{1,0:T(8,128)(2,1)}) custom-call(f32[2,8,264]{2,1,0:T(8,128)S(1)} %tables.1.tables_ref, f32[264,256]{1,0:T(8,128)} %get-tuple-element.18.own_hbm, f32[264,256]{1,0:T(8,128)S(1)} %collective-permute-done.3.come_ref, f32[1,256]{1,0:T(1,128)S(1)} %bitcast.11, f32[1,256]{1,0:T(1,128)S(1)} %bitcast.12), custom_call_target="tpu_custom_call" | custom-call | tf_op jit(solution)/shard_map/norm/pallas_call | solution.py:427
  (1 shorter events, 0.0 us)
Async XLA Ops:
  0.6 11.6 %copy-start.1 = (bf16[512,256]{1,0:T(8,128)(2,1)S(1)}, bf16[512,256]{1,0:T(8,128)(2,1)}, u32[]{:S(2)}) copy-start(bf16[512,256]{1,0:T(8,128)(2,1)} %q_ref.1) | copy-start | bytes 786436
  0.6 11.6 %copy-start.2 = (bf16[512,256]{1,0:T(8,128)(2,1)S(1)}, bf16[512,256]{1,0:T(8,128)(2,1)}, u32[]{:S(2)}) copy-start(bf16[512,256]{1,0:T(8,128)(2,1)} %k_ref.1) | copy-start | bytes 786436
  0.7 11.6 %copy-start.3 = (bf16[512,256]{1,0:T(8,128)(2,1)S(1)}, bf16[512,256]{1,0:T(8,128)(2,1)}, u32[]{:S(2)}) copy-start(bf16[512,256]{1,0:T(8,128)(2,1)} %v_ref.1) | copy-start | bytes 786436
  4.7 21.0 %collective-permute-start.1 = (bf16[1296,256]{1,0:T(8,128)(2,1)}, bf16[1296,256]{1,0:T(8,128)(2,1)S(1)}, u32[]{:S(2)}, u32[]{:S(2)}) collective-permute-start(bf16[1296,256]{1,0:T(8,128)(2,1)} %get-tuple-element.16), channel_id=1, source_target_pairs={{0,2},{1,3},{2,0},{3,1},{4,6},{5,7},{6,4},{7,5},{8,10},{9,11},{10,... | collective-permute-start | bytes 1990664 | tf_op jit(solution)/shard_map/ppermute | solution.py:444
  8.2 10.0 %collective-permute-start = (bf16[1,2,264,256]{3,2,1,0:T(8,128)(2,1)}, bf16[1,2,264,256]{3,2,1,0:T(8,128)(2,1)S(1)}, u32[]{:S(2)}, u32[]{:S(2)}) collective-permute-start(bf16[1,2,264,256]{3,2,1,0:T(8,128)(2,1)} %get-tuple-element.14), channel_id=1, source_target_pairs={{0,256},{8,264},{16,272},{24,280},{32,288},{40,296},{48,304},{56,3... | collective-permute-start | bytes 811016 | tf_op jit(solution)/shard_map/ppermute | solution.py:440
  19.0 23.2 %copy-start = (bf16[2048,256]{1,0:T(8,128)(2,1)S(1)}, bf16[2048,256]{1,0:T(8,128)(2,1)}, u32[]{:S(2)}) copy-start(bf16[2048,256]{1,0:T(8,128)(2,1)} %w_ref.1) | copy-start | bytes 3145732
  19.0 23.2 %copy-start.4 = (f32[256]{0:T(256)S(1)}, f32[256]{0:T(256)}, u32[]{:S(2)}) copy-start(f32[256]{0:T(256)} %param.28) | copy-start | bytes 3076
  19.0 23.1 %all-to-all-start = ((bf16[8,264,256]{2,1,0:T(8,128)(2,1)}), bf16[8,264,256]{2,1,0:T(8,128)(2,1)S(1)}, u32[]{:S(2)}, u32[]{:S(2)}) async-start(bf16[8,264,256]{2,1,0:T(8,128)(2,1)} %insert.1), calls=%async_computation | async-start | bytes 2162688 | tf_op jit(solution)/shard_map/all_to_all | solution.py:452
  25.8 16.4 %collective-permute-start.2 = (bf16[1296,256]{1,0:T(8,128)(2,1)S(1)}, bf16[1296,256]{1,0:T(8,128)(2,1)}, u32[]{:S(2)}, u32[]{:S(2)}) collective-permute-start(bf16[1296,256]{1,0:T(8,128)(2,1)S(1)} %collective-permute-done.1.packed_ref), channel_id=1, source_target_pairs={{0,8},{8,0},{16,24},{24,16},{32,40},{40,32},{48,56},{56,48},{64,72... | collective-permute-start | bytes 1990664 | tf_op jit(solution)/shard_map/ppermute | solution.py:448
  45.8 11.1 %all-to-all-start.1 = ((f32[8,2,264]{2,1,0:T(2,128)}), f32[8,2,264]{2,1,0:T(2,128)S(1)}, u32[]{:S(2)}, u32[]{:S(2)}) async-start(f32[8,2,264]{2,1,0:T(2,128)} %get-tuple-element.17), calls=%async_computation.1 | async-start | bytes 49152 | tf_op jit(solution)/shard_map/all_to_all | solution.py:452
  49.2 8.8 %copy-start.5 = (f32[256]{0:T(256)S(1)}, f32[256]{0:T(256)}, u32[]{:S(2)}) copy-start(f32[256]{0:T(256)} %param.30) | copy-start | bytes 3076
  49.2 8.8 %copy-start.6 = (f32[256]{0:T(256)S(1)}, f32[256]{0:T(256)}, u32[]{:S(2)}) copy-start(f32[256]{0:T(256)} %param.31) | copy-start | bytes 3076
  49.2 8.8 %collective-permute-start.3 = (f32[264,256]{1,0:T(8,128)}, f32[264,256]{1,0:T(8,128)S(1)}, u32[]{:S(2)}, u32[]{:S(2)}) collective-permute-start(f32[264,256]{1,0:T(8,128)} %get-tuple-element.19), channel_id=1, source_target_pairs={{0,2},{1,3},{2,0},{3,1},{4,6},{5,7},{6,4},{7,5},{8,10},{9,11},{10,... | collective-permute-start | bytes 811016 | tf_op jit(solution)/shard_map/ppermute | solution.py:444
